TPU v7x, 32 devices: a whole 2x2x4 slice. The times are simulated.
32 devices in a mesh: seq: 2 (over core), node: 4 (over y, x), group: 4 (over z).
Axes of the slice: x: 2, y: 2, z: 4, core: 2. Of those that a mesh axis runs over, the one named last changes fastest.
Arguments:
- patch_tokens: bfloat16 [64, 196, 384], P(('node', 'group'), 'seq'), may hold values from -6 to 6
- special_tokens: bfloat16 [64, 2, 384], P(('node', 'group')), may hold values from -6 to 6
- patch_upstream: bfloat16 [64, 196, 384], P(('node', 'group'), 'seq'), may hold values from -6 to 6
- special_upstream: bfloat16 [64, 2, 384], P(('node', 'group')), may hold values from -6 to 6
- patch_rank: int32 [64, 196], P(('node', 'group'), 'seq'), may hold values from 0 to 195, each once within a row
- keep_count: int32 [64], P(('node', 'group')), may hold values from 40 to 196
- project_in: float32 [384, 1152], replicated, may hold values from -0.3125 to 0.3125
- project_out: float32 [384, 384], replicated, may hold values from -1.25 to 1.25
- expand_weight: float32 [384, 1536], replicated, may hold values from -0.3125 to 0.3125
- reduce_weight: float32 [1536, 384], replicated, may hold values from -0.15625 to 0.15625
- small_params: float32 [12, 384], replicated
- project_in_momentum: float32 [384, 1152], replicated, may hold values from -0.75 to 0.75
- project_out_momentum: float32 [384, 384], replicated, may hold values from -0.75 to 0.75
- expand_momentum: float32 [384, 1536], replicated, may hold values from -0.75 to 0.75
- reduce_momentum: float32 [1536, 384], replicated, may hold values from -0.75 to 0.75
- small_momentum: float32 [12, 384], replicated, may hold values from -4 to 4
- project_in_error: float32 [32, 384, 1152], P(('seq', 'node', 'group')), may hold values from -96 to 96
- project_out_error: float32 [32, 384, 384], P(('seq', 'node', 'group')), may hold values from -96 to 96
- expand_error: float32 [32, 384, 1536], P(('seq', 'node', 'group')), may hold values from -96 to 96
- reduce_error: float32 [32, 1536, 384], P(('seq', 'node', 'group')), may hold values from -96 to 96
- project_in_factor: float32 [1152, 8], replicated, may hold values from -6 to 6
- project_out_factor: float32 [384, 8], replicated, may hold values from -6 to 6
- expand_factor: float32 [1536, 8], replicated, may hold values from -6 to 6
- reduce_factor: float32 [384, 8], replicated, may hold values from -6 to 6
Outputs:
- patch_output: bfloat16 [64, 196, 384], P(('node', 'group'), 'seq')
- special_output: bfloat16 [64, 2, 384], P(('node', 'group'))
- patch_grad: bfloat16 [64, 196, 384], P(('node', 'group'), 'seq')
- special_grad: bfloat16 [64, 2, 384], P(('node', 'group'))
- new_project_in: float32 [384, 1152], replicated
- new_project_out: float32 [384, 384], replicated
- new_expand: float32 [384, 1536], replicated
- new_reduce: float32 [1536, 384], replicated
- new_small: float32 [12, 384], replicated
- new_project_in_momentum: float32 [384, 1152], replicated
- new_project_out_momentum: float32 [384, 384], replicated
- new_expand_momentum: float32 [384, 1536], replicated
- new_reduce_momentum: float32 [1536, 384], replicated
- new_small_momentum: float32 [12, 384], replicated
- new_project_in_error: float32 [32, 384, 1152], P(('seq', 'node', 'group'))
- new_project_out_error: float32 [32, 384, 384], P(('seq', 'node', 'group'))
- new_expand_error: float32 [32, 384, 1536], P(('seq', 'node', 'group'))
- new_reduce_error: float32 [32, 1536, 384], P(('seq', 'node', 'group'))
- new_project_in_factor: float32 [1152, 8], replicated
- new_project_out_factor: float32 [384, 8], replicated
- new_expand_factor: float32 [1536, 8], replicated
- new_reduce_factor: float32 [384, 8], replicated
Inputs may be any that keep to these rules, and one draw needn't show every extreme that they name: `patch_rank`: the ranks of an image's patches are each of 0 to 195 once.
All inputs are finite; a program needn't handle non-finite values.
Results may differ from a plain program's by a relative error of at most 0.018.
Values may be sent and summed in bfloat16 or wider, within the bound.
A program may use at most 128 MiB of HBM per device.

v0:
```python
import math

import jax
import jax.numpy as jnp
from jax import lax
from jax.sharding import PartitionSpec as P

HEADS = 6
HEAD_DIM = 64


EPSILON = 1e-06
RATE = 0.1
DECAY = 0.9
HIGH = lax.Precision.HIGHEST


def shifted(block, axis, distance):
    devices = range(lax.axis_size(axis))
    route = [((i - distance) % len(devices), i) for i in devices]
    return lax.ppermute(block, axis, route)


def layer_norm(values, gain_row, bias_row):
    center = values - jnp.mean(values, axis=-1, keepdims=True)
    spread = jnp.mean(center * center, axis=-1, keepdims=True)
    return center * lax.rsqrt(spread + EPSILON) * gain_row + bias_row


def gelu_exact(values):
    return 0.5 * values * (1.0 + lax.erf(values * (1.0 / math.sqrt(2.0))))


def orthonormal(factor):
    columns = []
    for column_id in range(factor.shape[1]):
        column = factor[:, column_id]
        for earlier in columns:
            column = column - jnp.sum(earlier * column) * earlier
        columns.append(column * lax.rsqrt(jnp.sum(column * column) + EPSILON))
    return jnp.stack(columns, axis=1)


def matmul(left_side, right_side):
    return jnp.dot(left_side, right_side, preferred_element_type=jnp.float32)


def matmul_back(left_side, right_side):
    return lax.dot_general(
        left_side, right_side, (((1,), (1,)), ((), ())), preferred_element_type=jnp.float32
    )


def outer_sum(left_side, right_side):
    return lax.dot_general(
        left_side, right_side, (((0,), (0,)), ((), ())), preferred_element_type=jnp.float32
    )


def factor_right(merged, basis):
    return lax.dot_general(merged, basis, (((0,), (0,)), ((), ())), precision=HIGH)


def body(
    patch_tokens,
    special_tokens,
    patch_upstream,
    special_upstream,
    patch_rank,
    keep_count,
    project_in,
    project_out,
    expand_weight,
    reduce_weight,
    small_params,
    project_in_momentum,
    project_out_momentum,
    expand_momentum,
    reduce_momentum,
    small_momentum,
    project_in_error,
    project_out_error,
    expand_error,
    reduce_error,
    project_in_factor,
    project_out_factor,
    expand_factor,
    reduce_factor,
):
    image_count, half_rows, model_width = patch_tokens.shape
    length = half_rows + 2
    row_count = image_count * length
    scaling = 1.0 / math.sqrt(HEAD_DIM)
    first_half = lax.axis_index("seq") == 0
    kept_patches = patch_rank < keep_count[:, None]
    special_keep = jnp.ones((image_count, 2), jnp.bool_)
    keep_rows = jnp.concatenate([special_keep, kept_patches], axis=1)
    tokens_in = (
        jnp.concatenate([special_tokens, patch_tokens], axis=1).astype(jnp.float32)
        * keep_rows[..., None]
    )
    tokens_in = tokens_in.reshape(row_count, model_width)
    in_low = project_in.astype(jnp.bfloat16)
    out_low = project_out.astype(jnp.bfloat16)
    expand_low = expand_weight.astype(jnp.bfloat16)
    reduce_low = reduce_weight.astype(jnp.bfloat16)
    hidden_one = layer_norm(tokens_in, small_params[0], small_params[1]).astype(jnp.bfloat16)
    bias_qkv = jnp.concatenate(
        [small_params[2], jnp.zeros((model_width,), jnp.float32), small_params[3]]
    )
    qkv_low = (matmul(hidden_one, in_low) + bias_qkv).astype(jnp.bfloat16)
    qkv_low = qkv_low.reshape(image_count, length, 3, HEADS, HEAD_DIM)
    local_kv = qkv_low[:, 2:, 1:]
    remote_kv, remote_mask = shifted((local_kv, kept_patches.astype(jnp.bfloat16)), "seq", 1)
    remote_kept = remote_mask > 0.5
    lower_kv = jnp.where(first_half, local_kv, remote_kv)
    upper_kv = jnp.where(first_half, remote_kv, local_kv)
    all_kv = jnp.concatenate([qkv_low[:, :2, 1:], lower_kv, upper_kv], axis=1)
    key_mask = jnp.concatenate(
        [
            special_keep,
            jnp.where(first_half, kept_patches, remote_kept),
            jnp.where(first_half, remote_kept, kept_patches),
        ],
        axis=1,
    )
    query_rows = qkv_low[:, :, 0]
    key_rows = all_kv[:, :, 0]
    value_rows = all_kv[:, :, 1]

    def score_block(queries, keys_block, mask_block):
        raw_scores = (
            jnp.einsum("iqhd,ikhd->ihqk", queries, keys_block, preferred_element_type=jnp.float32)
            * scaling
        )
        return jnp.where(mask_block[:, None, None, :], raw_scores, -1e30)

    scores = score_block(query_rows, key_rows, key_mask)
    row_top = jnp.max(scores, axis=-1, keepdims=True)
    exp_scores = jnp.exp(scores - row_top)
    exp_total = jnp.sum(exp_scores, axis=-1, keepdims=True)
    probs_low = (exp_scores / exp_total).astype(jnp.bfloat16)
    log_total = row_top + jnp.log(exp_total)
    attended = jnp.einsum(
        "ihqk,ikhd->iqhd", probs_low, value_rows, preferred_element_type=jnp.float32
    )
    attended = attended.astype(jnp.bfloat16).reshape(row_count, model_width)
    middle = tokens_in + matmul(attended, out_low) + small_params[4]
    hidden_two = layer_norm(middle, small_params[5], small_params[6]).astype(jnp.bfloat16)
    pre_act = matmul(hidden_two, expand_low) + small_params[8:].reshape(-1)
    activated = gelu_exact(pre_act).astype(jnp.bfloat16)
    output = middle + matmul(activated, reduce_low) + small_params[7]
    out_rows = output.astype(jnp.bfloat16).reshape(image_count, length, model_width)
    weighting = jnp.concatenate(
        [
            jnp.full((image_count, 2), 0.5, jnp.float32),
            jnp.ones((image_count, half_rows), jnp.float32),
        ],
        axis=1,
    ).reshape(row_count, 1)
    upstream = (
        jnp.concatenate([special_upstream, patch_upstream], axis=1)
        .astype(jnp.float32)
        .reshape(row_count, model_width)
        * weighting
    )
    upstream_low = upstream.astype(jnp.bfloat16)
    grad_reduce = outer_sum(activated, upstream_low)
    grad_last_bias = jnp.sum(upstream, axis=0)
    grad_act = matmul_back(upstream_low, reduce_low).astype(jnp.bfloat16)
    gelu_value, gelu_pull = jax.vjp(gelu_exact, pre_act)
    grad_pre = gelu_pull(grad_act.astype(jnp.float32))[0].astype(jnp.bfloat16)
    grad_expand = outer_sum(hidden_two, grad_pre)
    grad_expand_bias = jnp.sum(grad_pre.astype(jnp.float32), axis=0)
    grad_hidden_two = matmul_back(grad_pre, expand_low)
    norm_value_two, norm_pull_two = jax.vjp(layer_norm, middle, small_params[5], small_params[6])
    grad_middle_norm, grad_gain_two, grad_shift_two = norm_pull_two(grad_hidden_two)
    grad_middle = upstream + grad_middle_norm
    grad_branch = grad_middle.astype(jnp.bfloat16)
    grad_project_out = outer_sum(attended, grad_branch)
    grad_out_bias = jnp.sum(grad_branch.astype(jnp.float32), axis=0)
    grad_attended = matmul_back(grad_branch, out_low).astype(jnp.bfloat16)
    grad_heads = grad_attended.reshape(image_count, length, HEADS, HEAD_DIM)
    scores = score_block(query_rows, key_rows, key_mask)
    probs_full = jnp.where(key_mask[:, None, None, :], jnp.exp(scores - log_total), 0.0)
    probs_low = probs_full.astype(jnp.bfloat16)
    grad_probs = jnp.einsum(
        "iqhd,ikhd->ihqk", grad_heads, value_rows, preferred_element_type=jnp.float32
    )
    row_delta = jnp.sum(probs_full * grad_probs, axis=-1, keepdims=True)
    grad_scores = (probs_full * (grad_probs - row_delta)).astype(jnp.bfloat16)
    grad_query = (
        jnp.einsum("ihqk,ikhd->iqhd", grad_scores, key_rows, preferred_element_type=jnp.float32)
        * scaling
    )
    grad_keys = (
        jnp.einsum("ihqk,iqhd->ikhd", grad_scores, query_rows, preferred_element_type=jnp.float32)
        * scaling
    )
    grad_values = jnp.einsum(
        "ihqk,iqhd->ikhd", probs_low, grad_heads, preferred_element_type=jnp.float32
    )
    grad_kv = jnp.stack([grad_keys, grad_values], axis=2)
    lower_grad = grad_kv[:, 2 : 2 + half_rows]
    upper_grad = grad_kv[:, 2 + half_rows :]
    own_grad = jnp.where(first_half, lower_grad, upper_grad)
    other_grad = jnp.where(first_half, upper_grad, lower_grad)
    own_grad = own_grad + shifted(other_grad, "seq", -1)
    special_qkv = jnp.concatenate([grad_query[:, :2, None], grad_kv[:, :2]], axis=2)
    special_sum = lax.psum(special_qkv, "seq")
    special_low = special_sum.astype(jnp.bfloat16) * 0.5
    patch_qkv = jnp.concatenate([grad_query[:, 2:, None], own_grad], axis=2).astype(jnp.bfloat16)
    grad_qkv = jnp.concatenate([special_low, patch_qkv], axis=1).reshape(row_count, 3 * model_width)
    grad_project_in = outer_sum(hidden_one, grad_qkv)
    grad_qkv_sum = jnp.sum(grad_qkv.astype(jnp.float32), axis=0)
    grad_hidden_one = matmul_back(grad_qkv, in_low)
    norm_value_one, norm_pull_one = jax.vjp(layer_norm, tokens_in, small_params[0], small_params[1])
    grad_in_norm, grad_gain_one, grad_shift_one = norm_pull_one(grad_hidden_one)
    grad_in = (grad_middle + grad_in_norm).reshape(image_count, length, model_width) * keep_rows[
        ..., None
    ]
    grad_small = jnp.concatenate(
        [
            jnp.stack(
                [
                    grad_gain_one,
                    grad_shift_one,
                    grad_qkv_sum[:model_width],
                    grad_qkv_sum[2 * model_width :],
                    grad_out_bias,
                    grad_gain_two,
                    grad_shift_two,
                    grad_last_bias,
                ]
            ),
            grad_expand_bias.reshape(-1, model_width),
        ],
        axis=0,
    )
    grads = (grad_project_in, grad_project_out, grad_expand, grad_reduce)
    errors = (project_in_error[0], project_out_error[0], expand_error[0], reduce_error[0])
    factors = (project_in_factor, project_out_factor, expand_factor, reduce_factor)
    merged = [grads[which] + errors[which] for which in range(4)]
    left_parts = [jnp.dot(merged[which], factors[which], precision=HIGH) for which in range(4)]
    workers = lax.axis_size("seq") * lax.axis_size("node") * lax.axis_size("group")
    first_sum, second_sum, third_sum, fourth_sum, small_sum = lax.psum(
        (left_parts[0], left_parts[1], left_parts[2], left_parts[3], grad_small), ("seq", "node")
    )
    left_sums = lax.psum((first_sum, second_sum, third_sum, fourth_sum, small_sum), "group")
    basis_list = [orthonormal(left_sums[which] / workers) for which in range(4)]
    right_parts = [factor_right(merged[which], basis_list[which]) for which in range(4)]
    first_sum, second_sum, third_sum, fourth_sum = (
        lax.psum(right_parts[0].astype(jnp.bfloat16), ("seq", "node")).astype(jnp.float32),
        lax.psum(right_parts[1].astype(jnp.bfloat16), ("seq", "node")).astype(jnp.float32),
        lax.psum(right_parts[2].astype(jnp.bfloat16), ("seq", "node")).astype(jnp.float32),
        lax.psum(right_parts[3].astype(jnp.bfloat16), ("seq", "node")).astype(jnp.float32),
    )
    right_sums = lax.psum((first_sum, second_sum, third_sum, fourth_sum), "group")
    weights = (project_in, project_out, expand_weight, reduce_weight)
    momenta = (project_in_momentum, project_out_momentum, expand_momentum, reduce_momentum)
    new_weights = []
    new_momenta = []
    new_errors = []
    new_factors = []
    for which in range(4):
        right_mean = right_sums[which] / workers
        approx = jnp.dot(basis_list[which], right_mean.T, precision=HIGH)
        new_errors.append((merged[which] - approx)[None])
        momentum_next = DECAY * momenta[which] + approx
        new_momenta.append(momentum_next)
        new_weights.append(weights[which] - RATE * momentum_next)
        new_factors.append(right_mean)
    small_next = DECAY * small_momentum + left_sums[4] / workers
    small_new = small_params - RATE * small_next
    return (
        out_rows[:, 2:],
        out_rows[:, :2],
        grad_in[:, 2:].astype(jnp.bfloat16),
        (2.0 * grad_in[:, :2]).astype(jnp.bfloat16),
        new_weights[0],
        new_weights[1],
        new_weights[2],
        new_weights[3],
        small_new,
        new_momenta[0],
        new_momenta[1],
        new_momenta[2],
        new_momenta[3],
        small_next,
        new_errors[0],
        new_errors[1],
        new_errors[2],
        new_errors[3],
        new_factors[0],
        new_factors[1],
        new_factors[2],
        new_factors[3],
    )


def solution(mesh):
    placed = (
        P(("node", "group"), "seq", None),
        P(("node", "group"), None, None),
        P(("node", "group"), "seq", None),
        P(("node", "group"), None, None),
        P(("node", "group"), "seq"),
        P(("node", "group")),
        P(),
        P(),
        P(),
        P(),
        P(),
        P(),
        P(),
        P(),
        P(),
        P(),
        P(("seq", "node", "group"), None, None),
        P(("seq", "node", "group"), None, None),
        P(("seq", "node", "group"), None, None),
        P(("seq", "node", "group"), None, None),
        P(),
        P(),
        P(),
        P(),
    )
    return jax.shard_map(
        body,
        mesh=mesh,
        in_specs=placed,
        out_specs=(
            P(("node", "group"), "seq", None),
            P(("node", "group"), None, None),
            P(("node", "group"), "seq", None),
            P(("node", "group"), None, None),
            P(),
            P(),
            P(),
            P(),
            P(),
            P(),
            P(),
            P(),
            P(),
            P(),
            P(("seq", "node", "group"), None, None),
            P(("seq", "node", "group"), None, None),
            P(("seq", "node", "group"), None, None),
            P(("seq", "node", "group"), None, None),
            P(),
            P(),
            P(),
            P(),
        ),
        check_vma=False,
    )
```

profile of v0, /device:TPU:0, one launch (start us, length us, event | category | flops | bytes accessed | tf_op | source)
XLA Modules:
  0.0 552.3 jit_solution(7482055090862508113)
XLA Ops:
  15.6 4.0 reshape.340
  32.3 2.0 fusion.55
  34.7 2.3 multiply_convert_fusion.1
  37.0 2.1 convert_reduce_fusion
  42.6 2.3 reshape.341
  44.9 2.3 copy.110
  47.2 2.1 convolution_bitcast_fusion
  54.6 2.0 broadcast_select_fusion
  60.4 10.9 %psum.133 = bf16[4,2,3,6,64]{1,4,3,0,2:T(8,128)(2,1)} all-reduce(f32[4,2,3,6,64]{1,4,3,0,2:T(8,128)} %pad_maximum_fusion), channel_id=1, replica_groups=mesh['seq'=2,'node'=4,'group'=4] {'seq'}, use_global_device_ids=true, to_apply=%region_9.10 | all-reduce | flops 9216 | bytes 55296 | tf_op jit(solution)/shard_map/psum | solution.py:210
  71.3 2.5 convert_multiply_fusion.2
  74.9 2.4 fusion.57
  77.3 2.6 fusion.58
  80.0 4.3 convolution_add_fusion.3
  84.3 4.5 fusion.59
  88.8 2.4 add_convert_fusion
  93.2 3.3 copy.112
  96.5 13.1 %reshape.331 = bf16[400,1152]{0,1:T(8,128)(2,1)} reshape(bf16[4,100,3,6,64]{1,0,4,3,2:T(4,128)(2,1)} %copy.112) | data formatting | bytes 1843200 | tf_op jit(solution)/shard_map/reshape | solution.py:213
  109.6 3.1 multiply_reduce_fusion.4
  114.1 2.0 reshape.332
  116.1 2.3 add_convert_fusion.1
  119.4 3.8 convolution_add_fusion.1
  123.1 3.7 fusion.56
  128.2 3.6 fusion.18
  134.3 49.5 %all-reduce.9.cloned.1.call-done = (f32[384,8]{0,1:T(8,128)}, f32[384,8]{0,1:T(8,128)}, f32[384,8]{0,1:T(8,128)}, f32[1536,8]{0,1:T(8,128)}, f32[12,384]{1,0:T(8,128)}) async-done(((f32[384,8]{0,1:T(8,128)}, f32[384,8]{0,1:T(8,128)}, f32[384,8]{0,1:T(8,128)}, f32[1536,8]{0,1:T(8,128)}, f32[12,384]{1,0:T(8,128)}), (f32[384,8]{0,1:T(8,128)}, f32[384,8]{0,1:T(8,128)}, f32[384,8]{0,1:T(8,128)}, ...) | async-done | bytes 104464 | tf_op jit(solution)/shard_map/psum | solution.py:246
  187.2 34.2 %all-reduce.11.cloned.1.call-done = (f32[384,8]{0,1:T(8,128)}, f32[384,8]{0,1:T(8,128)}, f32[384,8]{0,1:T(8,128)}, f32[1536,8]{0,1:T(8,128)}) async-done(((f32[384,8]{0,1:T(8,128)}, f32[384,8]{0,1:T(8,128)}, f32[384,8]{0,1:T(8,128)}, f32[1536,8]{0,1:T(8,128)}), (f32[384,8]{0,1:T(8,128)}, f32[384,8]{0,1:T(8,128)}, f32[384,8]{0,1:T(8,128)}, f32[1536,8]{0,1:T(8,128)})) %all-reduce.11.cloned.1.call-update) | async-done | bytes 86032 | tf_op jit(solution)/shard_map/psum | solution.py:249
  228.9 5.0 multiply_reduce_fusion.51
  238.3 6.1 %multiply_reduce_fusion.50 = (f32[]{:T(128)}, f32[]{:T(128)}, f32[]{:T(128)}, f32[]{:T(128)}, f32[]{:T(128)}, /*index=5*/f32[384]{0:T(512)S(1)}, f32[384]{0:T(512)S(1)}, f32[384]{0:T(512)S(1)}, f32[384]{0:T(512)S(1)}) fusion(f32[384]{0:T(512)S(1)} %get-tuple-element.367, f32[384]{0:T(512)S(1)} %get-tuple-element.366, f32[]{:T(128)} %get-tuple-element.365, ...), kind=kLoop, calls=%fused_computation.223 | loop fusion | flops 10747 | bytes 18488 | tf_op jit(solution)/shard_map/reduce_sum | solution.py:39
  245.1 3.8 multiply_reduce_fusion.49
  253.3 3.9 multiply_reduce_fusion.48
  257.9 2.6 multiply_reduce_fusion.47
  260.5 2.5 multiply_reduce_fusion.53
  263.6 2.6 multiply_reduce_fusion.46
  270.7 5.1 multiply_reduce_fusion.86
  280.4 6.5 %multiply_reduce_fusion.85 = (f32[]{:T(128)}, f32[]{:T(128)}, f32[]{:T(128)}, f32[]{:T(128)}, f32[]{:T(128)}, /*index=5*/f32[384]{0:T(512)S(1)}, f32[384]{0:T(512)S(1)}, f32[384]{0:T(512)S(1)}, f32[384]{0:T(512)S(1)}) fusion(f32[384]{0:T(512)S(1)} %get-tuple-element.397, f32[384]{0:T(512)S(1)} %get-tuple-element.396, f32[]{:T(128)} %get-tuple-element.395, ...), kind=kLoop, calls=%fused_computation.285 | loop fusion | flops 10747 | bytes 18488 | tf_op jit(solution)/shard_map/reduce_sum | solution.py:39
  287.5 3.8 multiply_reduce_fusion.84
  295.6 3.7 multiply_reduce_fusion.83
  299.9 2.5 multiply_reduce_fusion.82
  302.5 2.5 multiply_reduce_fusion.88
  305.6 2.4 multiply_reduce_fusion.81
  310.0 17.7 %subtract_multiply_fusion.14 = (f32[384,1]{0,1:T(1,128)S(1)}, f32[384,1]{0,1:T(1,128)S(1)}, f32[384,1]{0,1:T(1,128)S(1)}, f32[384,1]{0,1:T(1,128)S(1)}, f32[384,...) fusion(f32[384,1]{0,1:T(1,128)S(1)} %get-tuple-element.470, f32[384,8]{0,1:T(8,128)S(1)} %broadcast_multiply_fusion.7, ...), kind=kLoop, calls=%fused_computation.416 | loop fusion | flops 24192 | bytes 23180 | tf_op jit(solution)/shard_map/mul | solution.py:40
  332.2 5.1 multiply_reduce_fusion.121
  341.8 6.5 %multiply_reduce_fusion.120 = (f32[]{:T(128)}, f32[]{:T(128)}, f32[]{:T(128)}, f32[]{:T(128)}, f32[]{:T(128)}, /*index=5*/f32[384]{0:T(512)S(1)}, f32[384]{0:T(512)S(1)}, f32[384]{0:T(512)S(1)}, f32[384]{0:T(512)S(1)}) fusion(f32[384]{0:T(512)S(1)} %get-tuple-element.427, f32[384]{0:T(512)S(1)} %get-tuple-element.426, f32[]{:T(128)} %get-tuple-element.425, ...), kind=kLoop, calls=%fused_computation.347 | loop fusion | flops 10747 | bytes 18488 | tf_op jit(solution)/shard_map/reduce_sum | solution.py:39
  349.0 3.8 multiply_reduce_fusion.119
  357.1 3.7 multiply_reduce_fusion.118
  361.5 2.4 multiply_reduce_fusion.117
  363.9 2.4 multiply_reduce_fusion.123
  367.0 2.5 multiply_reduce_fusion.116
  371.4 17.8 %subtract_multiply_fusion.21 = (f32[384,1]{0,1:T(1,128)S(1)}, f32[384,1]{0,1:T(1,128)S(1)}, f32[384,1]{0,1:T(1,128)S(1)}, f32[384,1]{0,1:T(1,128)S(1)}, f32[384,...) fusion(f32[384,1]{0,1:T(1,128)S(1)} %get-tuple-element.432, f32[384,8]{0,1:T(8,128)S(1)} %broadcast_multiply_fusion.8, ...), kind=kLoop, calls=%fused_computation.424 | loop fusion | flops 24192 | bytes 23180 | tf_op jit(solution)/shard_map/mul | solution.py:40
  389.2 2.5 convolution_convert_fusion.2
  391.7 17.6 %subtract_multiply_fusion.7 = (f32[384,1]{0,1:T(1,128)S(1)}, f32[384,1]{0,1:T(1,128)S(1)}, f32[384,1]{0,1:T(1,128)S(1)}, f32[384,1]{0,1:T(1,128)S(1)}, f32[384,1...) fusion(f32[384,1]{0,1:T(1,128)S(1)} %get-tuple-element.372, f32[384,8]{0,1:T(8,128)S(1)} %broadcast_multiply_fusion.5, ...), kind=kLoop, calls=%fused_computation.408 | loop fusion | flops 24192 | bytes 23180 | tf_op jit(solution)/shard_map/mul | solution.py:40
  414.7 5.2 multiply_reduce_fusion.15
  424.3 6.5 %multiply_reduce_fusion.14 = (f32[]{:T(128)}, f32[]{:T(128)}, f32[]{:T(128)}, f32[]{:T(128)}, f32[]{:T(128)}, /*index=5*/f32[1536]{0:T(1024)S(1)}, f32[1536]{0:T(1024)S(1)}, f32[1536]{0:T(1024)S(1)}, f32[1536]{0:T(1024)S(1)}) fusion(f32[1536]{0:T(1024)S(1)} %get-tuple-element.339, f32[]{:T(128)S(6)} %rsqrt.150, f32[1536]{0:T(1024)S(1)} %get-tuple-element.337, ...), kind=kLoop, calls=%fused_computation.137 | loop fusion | flops 44539 | bytes 73788 | tf_op jit(solution)/shard_map/reduce_sum | solution.py:39
  431.6 3.8 multiply_reduce_fusion.13
  435.4 2.6 multiply_reduce_fusion.30
  438.6 5.0 multiply_reduce_fusion.12
  447.4 1.9 multiply_reduce_fusion.17
  453.7 18.0 %subtract_multiply_fusion = (f32[1536,1]{0,1:T(1,128)S(1)}, f32[1536,1]{0,1:T(1,128)S(1)}, f32[1536,1]{0,1:T(1,128)S(1)}, f32[1536,1]{0,1:T(1,128)S(1)}, f32[153...) fusion(f32[1536,1]{0,1:T(1,128)S(1)} %get-tuple-element.342, ...), kind=kLoop, calls=%fused_computation.190 | loop fusion | flops 96768 | bytes 92300 | tf_op jit(solution)/shard_map/mul | solution.py:40
  471.8 3.0 convolution_convert_fusion.5
  474.7 28.0 %all-reduce.4 = (bf16[1152,8]{0,1:T(8,128)(2,1)S(1)}, bf16[384,8]{0,1:T(8,128)(2,1)S(1)}, bf16[1536,8]{0,1:T(8,128)(2,1)S(1)}, bf16[384,8]{0,1:T(8,128)(2,1)S(1)}) all-reduce(bf16[1152,8]{0,1:T(8,128)(2,1)S(1)} %convolution_convert_fusion.2, ...), channel_id=1, replica_groups=mesh['seq'=2,'node'=4,'group'=4] {'seq','node'}, use_global_device_ids=true, to_apply=%region_50.51 | all-reduce | flops 27648 | bytes 110592 | tf_op jit(solution)/shard_map/psum | solution.py:253
  502.8 20.5 %all-reduce.12 = (f32[1152,8]{0,1:T(8,128)S(1)}, f32[384,8]{0,1:T(8,128)S(1)}, f32[1536,8]{0,1:T(8,128)S(1)}, f32[384,8]{0,1:T(8,128)S(1)}, f32[12,384]{1,0:T(8,128)S(1)}) all-reduce(bf16[1152,8]{0,1:T(8,128)(2,1)S(1)} %get-tuple-element.300, ...), channel_id=1, replica_groups=mesh['seq'=2,'node'=4,'group'=4] {'group'}, use_global_device_ids=true, to_apply=%region_51.52 | all-reduce | flops 32256 | bytes 202752 | tf_op jit(solution)/shard_map/psum | solution.py:258
  524.1 3.6 multiply_subtract_fusion.3
  527.7 5.9 %multiply_subtract_fusion.2 = (f32[384,1152]{1,0:T(8,128)}, f32[384,1152]{1,0:T(8,128)}, f32[1,384,1152]{2,1,0:T(8,128)}) fusion(f32[384,1152]{1,0:T(8,128)S(1)} %copy-done.9, f32[384,1152]{1,0:T(8,128)S(1)} %copy-done.37, f32[384,1152]{1,0:T(8,128)} %convolution_add_fusion.1, f32[384,8]{0,1:T(8,128)S(1)} %stack.25, f32[1152,8]{0,1:T(8,128)S(1)} %broadcast_multiply_fusion.3), kind=kOutput, calls=%fused_computation.40 | convolution fusion | flops 44679168 | bytes 10665984 | tf_op jit(solution)/shard_map/dot_general | solution.py:267
  533.6 6.0 %multiply_subtract_fusion = (f32[1536,384]{1,0:T(8,128)}, f32[1536,384]{1,0:T(8,128)}, f32[1,1536,384]{2,1,0:T(8,128)}) fusion(f32[1536,384]{1,0:T(8,128)S(1)} %copy-done.20, f32[1536,384]{1,0:T(8,128)S(1)} %copy-done.35, f32[1536,384]{1,0:T(8,128)} %convolution_add_fusion.3, f32[1536,8]{0,1:T(8,128)S(1)} %stack.28, f32[384,8]{0,1:T(8,128)S(1)} %broadcast_multiply_fusion.4), kind=kOutput, calls=%fused_computation.32 | convolution fusion | flops 59572224 | bytes 14217216 | tf_op jit(solution)/shard_map/dot_general | solution.py:267
  539.7 5.6 %multiply_subtract_fusion.1 = (f32[384,1536]{1,0:T(8,128)}, f32[384,1536]{1,0:T(8,128)}, f32[1,384,1536]{2,1,0:T(8,128)}) fusion(f32[384,1536]{1,0:T(8,128)S(1)} %copy-done.7, f32[384,1536]{1,0:T(8,128)S(1)} %copy-done.36, f32[384,1536]{1,0:T(8,128)S(1)} %convolution_add_fusion.4, f32[384,8]{0,1:T(8,128)S(1)} %stack.27, ...), kind=kOutput, calls=%fused_computation.34 | convolution fusion | flops 59572224 | bytes 14217216 | tf_op jit(solution)/shard_map/dot_general | solution.py:267
  (260 shorter events, 97.7 us)
Async XLA Ops:
  7.2 70.1 %copy-start = (f32[1536,8]{0,1:T(8,128)S(1)}, f32[1536,8]{0,1:T(8,128)}, u32[]{:S(2)}) copy-start(f32[1536,8]{0,1:T(8,128)} %param.46) | copy-start | bytes 147460
  7.2 6.7 %copy-start.8 = (f32[384,1152]{1,0:T(8,128)S(1)}, f32[384,1152]{1,0:T(8,128)}, u32[]{:S(2)}) copy-start(f32[384,1152]{1,0:T(8,128)} %param.30) | copy-start | bytes 5308420
  7.2 176.6 %all-reduce.9.cloned.1.call-start = ((), (), s32[]{:S(2)}) async-start(), calls=%async_computation | async-start | bytes 221184 | tf_op jit(solution)/shard_map/psum | solution.py:246
  8.1 18.2 %collective-permute-start.1 = (bf16[4,98]{1,0:T(4,128)(2,1)S(1)}, bf16[4,98]{1,0:T(4,128)(2,1)S(1)}, u32[]{:S(2)}, u32[]{:S(2)}) collective-permute-start(bf16[4,98]{1,0:T(4,128)(2,1)S(1)} %get-tuple-element.441), channel_id=1, source_target_pairs={{16,0},{0,16},{17,1},{1,17},{18,2},{2,18},{19,3},{3,19},{20,4},{4,... | collective-permute-start | bytes 2360 | tf_op jit(solution)/shard_map/ppermute | solution.py:21
  13.8 10.3 %copy-start.10 = (f32[400,384]{1,0:T(8,128)}, f32[400,384]{1,0:T(8,128)S(1)}, u32[]{:S(2)}) copy-start(f32[400,384]{1,0:T(8,128)S(1)} %reshape.338) | copy-start | bytes 1843204
  21.3 2.6 copy-start.55
  21.3 2.6 copy-start.39
  21.3 2.8 copy-start.45
  21.3 3.1 slice-start.1
  23.1 3.4 collective-permute-start
  23.9 1.9 slice-start
  24.4 2.1 copy-start.33
  26.3 2.5 copy-start.31
  28.9 1.4 copy-start.13
  32.3 2.3 copy-start.6
  34.7 2.3 copy-start.19
  34.7 2.3 copy-start.21
  34.7 2.3 copy-start.54
  39.1 1.0 copy-start.24
  40.1 1.4 copy-start.23
  40.7 0.8 copy-start.15
  47.2 2.1 copy-start.14
  47.2 2.1 copy-start.29
  49.3 4.3 copy-start.2
  51.5 1.0 copy-start.32
  52.5 6.2 %copy-start.26 = (f32[4,100,6,64]{1,3,2,0:T(8,128)}, f32[4,100,6,64]{1,3,2,0:T(8,128)S(1)}, u32[]{:S(2)}) copy-start(f32[4,100,6,64]{1,3,2,0:T(8,128)S(1)} %fusion.11) | copy-start | bytes 1843204
  53.4 1.1 copy-start.4
  53.4 3.2 copy-start.40
  54.6 2.0 copy-start.16
  54.6 2.0 copy-start.30
  54.6 3.2 copy-start.25
  54.6 3.2 copy-start.34
  71.3 2.6 copy-start.27
  71.3 3.6 copy-start.53
  73.8 15.0 %collective-permute-start.2 = (f32[4,98,2,6,64]{1,4,3,0,2:T(8,128)}, f32[4,98,2,6,64]{1,4,3,0,2:T(8,128)}, u32[]{:S(2)}, u32[]{:S(2)}) collective-permute-start(f32[4,98,2,6,64]{1,4,3,0,2:T(8,128)} %broadcast_select_fusion), channel_id=1, source_target_pairs={{16,0},{0,16},{17,1},{1,17},{18,2},{2,18},{19,3},{3,19},{20,4},{4,... | collective-permute-start | bytes 3612680 | tf_op jit(solution)/shard_map/ppermute | solution.py:21
  74.9 5.1 copy-start.12
  74.9 5.1 copy-start.22
  80.0 4.3 copy-start.52
  80.0 8.8 %copy-start.5 = (f32[4,198,1,6,64]{1,4,3,0,2:T(8,128)S(1)}, f32[4,198,1,6,64]{1,4,3,0,2:T(8,128)}, u32[]{:S(2)}) copy-start(f32[4,198,1,6,64]{1,4,3,0,2:T(8,128)} %copy-done.4) | copy-start | bytes 3649540
  84.3 4.5 copy-start.3
  88.8 2.4 copy-start.28
  88.8 2.4 copy-start.38
  109.6 3.1 copy-start.11
  109.6 3.5 copy-start.17
  112.7 3.4 copy-start.43
  119.3 3.8 copy-start.49
  128.1 93.3 %all-reduce.11.cloned.1.call-start = ((), (), s32[]{:S(2)}) async-start(), calls=%async_computation.1 | async-start | bytes 172032 | tf_op jit(solution)/shard_map/psum | solution.py:249
  131.7 196.1 %copy-start.18 = (f32[384,384]{1,0:T(8,128)S(1)}, f32[384,384]{1,0:T(8,128)}, u32[]{:S(2)}) copy-start(f32[384,384]{1,0:T(8,128)} %convolution_add_fusion.7) | copy-start | bytes 1769476
  328.9 81.8 %copy-start.48 = (f32[1536,8]{0,1:T(8,128)S(1)}, f32[1536,8]{0,1:T(8,128)}, u32[]{:S(2)}) copy-start(f32[1536,8]{0,1:T(8,128)} %get-tuple-element.299) | copy-start | bytes 147460
  410.7 92.1 %copy-start.50 = (f32[12,384]{1,0:T(8,128)S(1)}, f32[12,384]{1,0:T(8,128)}, u32[]{:S(2)}) copy-start(f32[12,384]{1,0:T(8,128)} %get-tuple-element.290) | copy-start | bytes 55300
  410.7 112.8 %copy-start.44 = (f32[12,384]{1,0:T(8,128)S(1)}, f32[12,384]{1,0:T(8,128)}, u32[]{:S(2)}) copy-start(f32[12,384]{1,0:T(8,128)} %param.34) | copy-start | bytes 55300
  410.7 112.8 %copy-start.51 = (f32[12,384]{1,0:T(8,128)S(1)}, f32[12,384]{1,0:T(8,128)}, u32[]{:S(2)}) copy-start(f32[12,384]{1,0:T(8,128)} %param.39) | copy-start | bytes 55300
  523.3 4.3 copy-start.9
  523.3 4.3 copy-start.37
  523.4 10.2 %copy-start.42 = (f32[1152,8]{0,1:T(8,128)}, f32[1152,8]{0,1:T(8,128)S(1)}, u32[]{:S(2)}) copy-start(f32[1152,8]{0,1:T(8,128)S(1)} %broadcast_multiply_fusion.3) | copy-start | bytes 110596
  523.4 10.2 %copy-start.46 = (f32[384,8]{0,1:T(8,128)}, f32[384,8]{0,1:T(8,128)S(1)}, u32[]{:S(2)}) copy-start(f32[384,8]{0,1:T(8,128)S(1)} %broadcast_multiply_fusion.6) | copy-start | bytes 36868
  523.4 10.2 %copy-start.47 = (f32[384,8]{0,1:T(8,128)}, f32[384,8]{0,1:T(8,128)S(1)}, u32[]{:S(2)}) copy-start(f32[384,8]{0,1:T(8,128)S(1)} %broadcast_multiply_fusion.4) | copy-start | bytes 36868
  523.4 16.2 %copy-start.41 = (f32[1536,8]{0,1:T(8,128)}, f32[1536,8]{0,1:T(8,128)S(1)}, u32[]{:S(2)}) copy-start(f32[1536,8]{0,1:T(8,128)S(1)} %broadcast_multiply_fusion.2) | copy-start | bytes 147460
  527.7 5.9 %copy-start.20 = (f32[1536,384]{1,0:T(8,128)S(1)}, f32[1536,384]{1,0:T(8,128)}, u32[]{:S(2)}) copy-start(f32[1536,384]{1,0:T(8,128)} %param.33) | copy-start | bytes 7077892
  527.7 5.9 %copy-start.35 = (f32[1536,384]{1,0:T(8,128)S(1)}, f32[1536,384]{1,0:T(8,128)}, u32[]{:S(2)}) copy-start(f32[1536,384]{1,0:T(8,128)} %param.38) | copy-start | bytes 7077892
  533.6 6.0 %copy-start.7 = (f32[384,1536]{1,0:T(8,128)S(1)}, f32[384,1536]{1,0:T(8,128)}, u32[]{:S(2)}) copy-start(f32[384,1536]{1,0:T(8,128)} %param.32) | copy-start | bytes 7077892
  533.6 6.0 %copy-start.36 = (f32[384,1536]{1,0:T(8,128)S(1)}, f32[384,1536]{1,0:T(8,128)}, u32[]{:S(2)}) copy-start(f32[384,1536]{1,0:T(8,128)} %param.37) | copy-start | bytes 7077892
  539.6 5.6 %copy-start.1 = (f32[1536,8]{0,1:T(8,128)S(1)}, f32[1536,8]{0,1:T(8,128)}, u32[]{:S(2)}) copy-start(f32[1536,8]{0,1:T(8,128)} %param.46) | copy-start | bytes 147460
Sparse Core Ops, SparseCore 0:
  128.2 55.5 all-reduce.8
  186.5 34.8 all-reduce.10
where the time goes:
time: 561 us; the launch traced here: 552 us
  other arithmetic  249 us (44%)
  waiting for transfers between devices  83.7 us (15%)
  matrix products  75.3 us (13%)
  blocking collectives  59.4 us (11%)
  local copies, waits for them, and re-layouts  47.5 us (8%)
  between operations  36.8 us (7%)
    reduce_sum x39, other arithmetic, orthonormal(): column = column - jnp.sum(earlier * column) * earlier  117 us
    mul x7, other arithmetic, orthonormal(): columns.append(column * lax.rsqrt(jnp.sum(column * column) + EPSILON))  71.1 us
    psum x1, waiting for transfers between devices, body(): lax.psum((left_parts[0], left_parts[1], left_parts[2], left_parts[3], gra...  49.5 us
    psum x1, waiting for transfers between devices, body(): lax.psum((first_sum, second_sum, third_sum, fourth_sum, small_sum), 'group')  34.2 us
    reduce_sum x17, other arithmetic, orthonormal(): columns.append(column * lax.rsqrt(jnp.sum(column * column) + EPSILON))  31.3 us
    psum x1, blocking collectives, body(): lax.psum(right_parts[0].astype(jnp.bfloat16), ('seq', 'node'))  28 us
    dot_general x4, matrix products, body(): approx = jnp.dot(basis_list[which], right_mean.T, precision=HIGH)  21.1 us
    psum x1, blocking collectives, body(): lax.psum((first_sum, second_sum, third_sum, fourth_sum), 'group')  20.5 us
  transfers between devices with their start and end apart: 5, of which 2 were waited for; matrix products, arithmetic and copies ran while one was open for 8% of the time, Pallas kernels for 0%

commit v1 on v0

v1 whole, which is shorter than its diff:
```python
import functools
import math

import jax
import jax.numpy as jnp
from jax import lax
from jax.experimental import pallas as pl
from jax.experimental.pallas import tpu as pltpu
from jax.sharding import PartitionSpec as P

HEADS = 6
HEAD_DIM = 64
EPSILON = 1e-06
RATE = 0.1
DECAY = 0.9
RANK = 8
MESH = pl.DeviceIdType.MESH
F32 = jnp.float32
BF16 = jnp.bfloat16
INPUTS = (
    "patch_tokens",
    "special_tokens",
    "patch_upstream",
    "special_upstream",
    "patch_rank",
    "keep_count",
    "project_in",
    "project_out",
    "expand_weight",
    "reduce_weight",
    "small_params",
    "project_in_momentum",
    "project_out_momentum",
    "expand_momentum",
    "reduce_momentum",
    "small_momentum",
    "project_in_error",
    "project_out_error",
    "expand_error",
    "reduce_error",
    "project_in_factor",
    "project_out_factor",
    "expand_factor",
    "reduce_factor",
)
OUTPUTS = (
    "out_patch",
    "out_special",
    "grad_patch",
    "grad_special",
    "new_in",
    "new_out",
    "new_exp",
    "new_red",
    "new_small",
    "mom_in",
    "mom_out",
    "mom_exp",
    "mom_red",
    "mom_small",
    "err_in",
    "err_out",
    "err_exp",
    "err_red",
    "new_f_in",
    "new_f_out",
    "new_f_exp",
    "new_f_red",
)
KEYS = 128


def round_up(value, unit):
    return -(-value // unit) * unit


def mm(left_side, right_side):
    return jnp.dot(left_side, right_side, preferred_element_type=F32)


def mm_nt(left_side, right_side):
    return lax.dot_general(
        left_side, right_side, (((1,), (1,)), ((), ())), preferred_element_type=F32
    )


def mm_tn(left_side, right_side):
    return lax.dot_general(
        left_side, right_side, (((0,), (0,)), ((), ())), preferred_element_type=F32
    )


def split(value):
    high = value.astype(BF16)
    return high, (value - high.astype(F32)).astype(BF16)


def orthonormal(rows):
    row_ids = lax.broadcasted_iota(jnp.int32, (RANK, 1), 0)
    for step in range(RANK):
        own = rows[step : step + 1, :]
        dots = jnp.sum(rows * own, axis=1, keepdims=True)
        scale = lax.rsqrt(dots[step : step + 1, :] + EPSILON)
        unit = own * scale
        later = jnp.where(row_ids > step, dots * scale, 0.0)
        rows = jnp.where(row_ids == step, unit, rows - later * unit)
    return rows


def outer_product(basis, right):
    basis_high, basis_low = split(basis)
    right_high, right_low = split(right)
    left_stack = jnp.concatenate(
        [basis_high.astype(F32), basis_low.astype(F32)] * 2, axis=0
    ).astype(BF16)
    right_stack = jnp.concatenate(
        [right_high.astype(F32)] * 2 + [right_low.astype(F32)] * 2, axis=0
    ).astype(BF16)
    return left_stack, right_stack


class Names:
    pass


def layer_kernel(chips, groups, images, half, names, *all_refs):
    refs = Names()
    for name, ref in zip(names, all_refs):
        setattr(refs, name, ref)
    r = refs
    width = HEADS * HEAD_DIM
    special = round_up(half, 8)
    block = round_up(special + 2, 16)
    rows_all = images * block
    workers = 2 * chips
    seq = lax.axis_index("seq")
    node = lax.axis_index("node")
    group = lax.axis_index("group")
    chip = node * groups + group
    partner = 1 - seq

    loads = {}

    def load(name, source, target):
        loads[name] = pltpu.make_async_copy(source, target, r.load_sem.at[len(loads)])
        loads[name].start()

    load("tokens", r.patch_tokens, r.raw_patch)
    load("special", r.special_tokens, r.raw_special)
    load("rank", r.patch_rank, r.rank)
    load("small", r.small_params, r.new_small)
    load("w_in", r.project_in, r.new_in)
    load("f_in", r.project_in_factor, r.new_f_in)
    load("f_out", r.project_out_factor, r.new_f_out)
    load("f_exp", r.expand_factor, r.new_f_exp)
    load("f_red", r.reduce_factor, r.new_f_red)
    load("upstream", r.patch_upstream, r.raw_up)
    load("special_up", r.special_upstream, r.raw_special_up)
    load("e_in", r.project_in_error.at[0], r.err_in)
    load("e_exp", r.expand_error.at[0], r.err_exp)
    load("e_red", r.reduce_error.at[0], r.err_red)
    load("e_out", r.project_out_error.at[0], r.err_out)
    load("w_out", r.project_out, r.new_out)
    load("w_exp", r.expand_weight, r.new_exp)
    load("w_red", r.reduce_weight, r.new_red)
    load("m_small", r.small_momentum, r.mom_small)
    load("m_out", r.project_out_momentum, r.mom_out)
    load("m_exp", r.expand_momentum, r.mom_exp)
    load("m_red", r.reduce_momentum, r.mom_red)
    load("m_in", r.project_in_momentum, r.mom_in)

    barrier = pltpu.get_barrier_semaphore()
    pl.semaphore_signal(barrier, inc=1, device_id={"seq": partner}, device_id_type=MESH)

    def peer_of(step):
        other = lax.rem(chip + step, chips)
        return other // groups, lax.rem(other, groups)

    def greet(step, carry):
        other_node, other_group = peer_of(step)
        pl.semaphore_signal(
            barrier,
            inc=1,
            device_id={"node": other_node, "group": other_group},
            device_id_type=MESH,
        )
        return carry

    lax.fori_loop(1, chips, greet, 0)

    def to_partner(source, target, sem_id):
        return pltpu.make_async_remote_copy(
            src_ref=source,
            dst_ref=target,
            send_sem=r.pair_send.at[sem_id],
            recv_sem=r.pair_recv.at[sem_id],
            device_id={"seq": partner},
            device_id_type=MESH,
        )

    def to_chip(step, source, target, sems, sem_id):
        other_node, other_group = peer_of(step)
        return pltpu.make_async_remote_copy(
            src_ref=source,
            dst_ref=target,
            send_sem=sems[0].at[sem_id, step],
            recv_sem=sems[1].at[sem_id, step],
            device_id={"node": other_node, "group": other_group},
            device_id_type=MESH,
        )

    chip_sems = (r.chip_send, r.chip_recv)

    def chips_start(source, slots, sem_id):
        slots[chip] = source[...]

        def go(step, carry):
            to_chip(step, source, slots.at[chip], chip_sems, sem_id).start()
            return carry

        lax.fori_loop(1, chips, go, 0)

    def chips_finish(source, slots, sem_id):
        def done(step, carry):
            to_chip(step, source, slots.at[chip], chip_sems, sem_id).wait()
            return carry

        lax.fori_loop(1, chips, done, 0)

        def add(index, total):
            return total + slots[index].astype(F32)

        return lax.fori_loop(1, chips, add, slots[0].astype(F32), unroll=min(chips - 1, 15))

    def along(axis, step):
        size = lax.axis_size(axis)
        return {axis: lax.rem(lax.axis_index(axis) + step, size)}

    def axis_copy(axis, step, source, slots, sem_id):
        return pltpu.make_async_remote_copy(
            src_ref=source,
            dst_ref=slots.at[lax.axis_index(axis)],
            send_sem=r.chip_send.at[sem_id, step],
            recv_sem=r.chip_recv.at[sem_id, step],
            device_id=along(axis, step),
            device_id_type=MESH,
        )

    def axis_start(axis, source, slots, sem_id):
        slots[lax.axis_index(axis)] = source[...]

        def go(step, carry):
            axis_copy(axis, step, source, slots, sem_id).start()
            return carry

        lax.fori_loop(1, lax.axis_size(axis), go, 0)

    def axis_finish(axis, source, slots, sem_id):
        def done(step, carry):
            axis_copy(axis, step, source, slots, sem_id).wait()
            return carry

        lax.fori_loop(1, lax.axis_size(axis), done, 0)
        total = slots[0].astype(F32)
        for index in range(1, lax.axis_size(axis)):
            total = total + slots[index].astype(F32)
        return total

    loads["rank"].wait()
    r.flags[...] = jnp.zeros_like(r.flags)
    for i in range(images):
        r.flags[i : i + 1, 0:half] = jnp.where(
            r.rank[i : i + 1, :] < r.keep_count[i], 1.0, 0.0
        ).astype(F32)
    lane_ids = lax.broadcasted_iota(jnp.int32, (1, KEYS), 1)
    special_lanes = jnp.where((lane_ids >= special) & (lane_ids < special + 2), 1.0, 0.0)
    own_columns = jnp.transpose(r.flags[...] + special_lanes)
    for i in range(images):
        r.mask_columns[i, 0:KEYS, :] = own_columns[:, i : i + 1]

    small = r.new_small
    loads["small"].wait()

    def small_row(index):
        return small[index : index + 1, :]

    loads["tokens"].wait()
    loads["special"].wait()
    r.mixed[...] = r.raw_patch[...].astype(F32)
    for i in range(images):
        base = i * block
        r.tokens[base + special - 8 : base + block, :] = jnp.zeros(
            (block - special + 8, width), F32
        )
        r.tokens[base : base + half, :] = (
            r.mixed[:, i, :] * r.mask_columns[i, 0:half, :]
        )
        r.tokens[base + special : base + special + 2, :] = r.raw_special[i].astype(F32)

    def normalise(source, i, gain, shift, xhat_ref, scale_ref, hidden_ref):
        at = pl.ds(pl.multiple_of(i * block, 16), block)
        values = source[at, :]
        center = values - jnp.mean(values, axis=1, keepdims=True)
        spread = jnp.mean(center * center, axis=1, keepdims=True)
        scale = lax.rsqrt(spread + EPSILON)
        xhat = center * scale
        xhat_ref[at, :] = xhat
        scale_ref[at, :] = scale
        hidden_ref[at, :] = (xhat * gain + shift).astype(BF16)

    @pl.loop(0, images)
    def _(i):
        normalise(r.tokens, i, small_row(0), small_row(1), r.xhat_one, r.scale_one, r.hidden_one)

    loads["w_in"].wait()
    r.low_in[...] = r.new_in[...].astype(BF16)
    for i in range(images):
        r.keys[0, i, block:KEYS, :] = jnp.zeros((KEYS - block, 2 * width), BF16)
    for part in (1, 2, 0):
        product = mm(r.hidden_one[...], r.low_in[:, part * width : (part + 1) * width])
        if part == 0:
            query = (product + small_row(2)).astype(BF16).astype(F32) * (
                1.0 / math.sqrt(HEAD_DIM)
            )
            r.query[...] = query.astype(BF16)
        else:
            if part == 2:
                product = product + small_row(3)
            for i in range(images):
                r.keys[0, i, 0:block, (part - 1) * width : part * width] = product[
                    i * block : (i + 1) * block
                ].astype(BF16)
        if part == 2:
            pl.semaphore_wait(barrier, chips)
            key_copy = to_partner(r.keys.at[0], r.keys.at[1], 0)
            flag_copy = to_partner(r.flags, r.other_flags, 1)
            key_copy.start()
            flag_copy.start()

    def error_left(error_ref, factor_ref, row_start, row_count):
        return mm_nt(
            factor_ref[...].astype(BF16), error_ref[row_start : row_start + row_count, :].astype(BF16)
        )

    loads["upstream"].wait()
    loads["special_up"].wait()
    r.mixed[...] = r.raw_up[...].astype(F32)
    for i in range(images):
        base = i * block
        r.middle[base + special - 8 : base + block, :] = jnp.zeros(
            (block - special + 8, width), F32
        )
        r.middle[base : base + half, :] = r.mixed[:, i, :]
        r.middle[base + special : base + special + 2, :] = 0.5 * r.raw_special_up[i].astype(F32)
    r.upstream[...] = r.middle[...].astype(BF16)
    loads["f_in"].wait()
    loads["f_out"].wait()
    loads["f_exp"].wait()
    loads["f_red"].wait()
    loads["e_in"].wait()
    r.left_in[...] = error_left(r.err_in, r.new_f_in, 0, width)
    loads["e_exp"].wait()
    r.lefts[4] = error_left(r.err_exp, r.new_f_exp, 0, width)
    loads["e_red"].wait()
    for part in range(4):
        r.lefts[part] = error_left(r.err_red, r.new_f_red, part * width, width)
    loads["e_out"].wait()
    r.lefts[5] = error_left(r.err_out, r.new_f_out, 0, width)

    key_copy.wait()
    flag_copy.wait()
    other_columns = jnp.transpose(r.other_flags[...])
    for i in range(images):
        r.mask_columns[i, KEYS : 2 * KEYS, :] = other_columns[:, i : i + 1]

    pair_width = 2 * HEAD_DIM
    pairs = HEADS // 2
    low_lanes = lax.broadcasted_iota(jnp.int32, (1, pair_width), 1) < HEAD_DIM

    def stacked(value):
        zero = jnp.zeros_like(value)
        return jnp.concatenate(
            [jnp.where(low_lanes, value, zero), jnp.where(low_lanes, zero, value)], axis=0
        )

    def unstacked(value):
        return jnp.where(low_lanes, value[0:block], value[block : 2 * block])

    def of_both(i, lanes):
        return jnp.concatenate([r.keys[0, i, :, lanes], r.keys[1, i, :, lanes]], axis=0)

    @pl.loop(0, images)
    def _(i):
        at = pl.ds(pl.multiple_of(i * block, 16), block)
        valid = r.mask_columns[i] > 0.5
        for pair in range(pairs):
            lanes = slice(pair * pair_width, (pair + 1) * pair_width)
            value_lanes = slice(width + pair * pair_width, width + (pair + 1) * pair_width)
            scores = mm_nt(of_both(i, lanes), stacked(r.query[at, lanes]))
            scores = jnp.where(valid, scores, -1e30)
            top = jnp.max(scores, axis=0, keepdims=True)
            weights = jnp.exp(scores - top)
            probs = weights * (1.0 / jnp.sum(weights, axis=0, keepdims=True))
            r.probs[i * pairs + pair] = probs
            mixed = mm_tn(probs.astype(BF16), of_both(i, value_lanes))
            r.attended[at, lanes] = unstacked(mixed).astype(BF16)

    loads["w_out"].wait()
    r.low_out[...] = r.new_out[...].astype(BF16)
    r.middle[...] = r.tokens[...] + mm(r.attended[...], r.low_out[...]) + small_row(4)

    @pl.loop(0, images)
    def _(i):
        normalise(r.middle, i, small_row(5), small_row(6), r.xhat_two, r.scale_two, r.hidden_two)

    strip = 16
    chunk = 2 * width
    hidden_lanes = r.low_exp.shape[1]
    loads["w_exp"].wait()
    r.low_exp[...] = r.new_exp[...].astype(BF16)
    loads["w_red"].wait()
    r.low_red[...] = r.new_red[...].astype(BF16)
    bias_rows = chunk // width
    r.total[...] = r.middle[...] + small_row(7)
    for part in range(hidden_lanes // chunk):
        lanes = slice(part * chunk, (part + 1) * chunk)
        bias = jnp.concatenate(
            [small_row(8 + part * bias_rows + index) for index in range(bias_rows)], axis=1
        )
        r.wide[...] = mm(r.hidden_two[...], r.low_exp[:, lanes])

        @pl.loop(0, rows_all // strip)
        def _(index):
            at = pl.ds(pl.multiple_of(index * strip, strip), strip)
            pre = r.wide[at, :] + bias
            normal = 0.5 + 0.5 * lax.erf(pre * (1.0 / math.sqrt(2.0)))
            density = jnp.exp(-0.5 * pre * pre) * (1.0 / math.sqrt(2.0 * math.pi))
            r.activated[at, lanes] = (pre * normal).astype(BF16)
            r.slope[at, lanes] = normal + pre * density

        r.total[...] += mm(r.activated[:, lanes], r.low_red[lanes, :])
    for i in range(images):
        base = i * block
        r.mixed[:, i, :] = r.total[base : base + half, :]
        r.out_special[i] = r.total[base + special : base + special + 2, :].astype(BF16)

    r.out_patch[...] = r.mixed[...].astype(BF16)

    folded = mm_nt(r.new_f_red[...].astype(BF16), r.upstream[...]).astype(BF16)
    for part in range(4):
        lanes = slice(part * width, (part + 1) * width)
        r.lefts[part] += mm(folded, r.activated[:, lanes])
    ones = jnp.ones((8, rows_all), BF16)
    for part in range(hidden_lanes // chunk):
        lanes = slice(part * chunk, (part + 1) * chunk)
        grad_act = mm_nt(r.upstream[...], r.low_red[lanes, :]).astype(BF16).astype(F32)
        grad_pre = grad_act * r.slope[:, lanes]
        r.grad_pre[:, lanes] = grad_pre.astype(BF16)
        row = jnp.sum(grad_pre, axis=0, keepdims=True)
        for index in range(bias_rows):
            first = 4 + part * bias_rows + index
            r.lefts[6, first : first + 1, :] = row[:, index * width : (index + 1) * width]
        back = mm_nt(r.grad_pre[:, lanes], r.low_exp[:, lanes])
        if part == 0:
            r.total[...] = back
        else:
            r.total[...] += back
    folded = mm_nt(r.new_f_exp[...].astype(BF16), r.grad_pre[...]).astype(BF16)
    r.lefts[4] += mm(folded, r.hidden_two[...])

    def normalise_back(i, gain, xhat_ref, scale_ref, gain_ref, shift_ref):
        at = pl.ds(pl.multiple_of(i * block, 16), block)
        grad = r.total[at, :]
        xhat = xhat_ref[at, :]
        gained = grad * gain
        first = jnp.mean(gained, axis=1, keepdims=True)
        second = jnp.mean(gained * xhat, axis=1, keepdims=True)
        gain_ref[...] += jnp.sum(grad * xhat, axis=0, keepdims=True)
        shift_ref[...] += jnp.sum(grad, axis=0, keepdims=True)
        return scale_ref[at, :] * (gained - first - xhat * second)

    r.gain_sum[...] = jnp.zeros_like(r.gain_sum)
    r.shift_sum[...] = jnp.zeros_like(r.shift_sum)

    @pl.loop(0, images)
    def _(i):
        at = pl.ds(pl.multiple_of(i * block, 16), block)
        back = normalise_back(i, small_row(5), r.xhat_two, r.scale_two, r.gain_sum, r.shift_sum)
        grad = r.upstream[at, :].astype(F32) + back
        r.grad_middle[at, :] = grad
        r.grad_branch[at, :] = grad.astype(BF16)

    r.lefts[6, 1:2, :] = r.gain_sum[...]
    r.lefts[6, 2:3, :] = r.shift_sum[...]
    r.lefts[6, 3:4, :] = mm(ones, r.upstream[...])[0:1]
    r.lefts[6, 0:1, :] = mm(ones, r.grad_branch[...])[0:1]
    r.lefts[7] = jnp.zeros((RANK, width), F32)
    folded = mm_nt(r.new_f_out[...].astype(BF16), r.grad_branch[...]).astype(BF16)
    r.lefts[5] += mm(folded, r.attended[...])

    def units_pair_start(units, arrived, sem_id):
        copy = to_partner(units, arrived, sem_id)
        copy.start()
        return copy

    def units_group_start(copy, units, arrived, outgoing, slots, sem_id):
        copy.wait()
        for index in range(2):
            first = seq * 4 + 2 * index
            outgoing[0, index] = jnp.concatenate(
                [units[first] + arrived[first], units[first + 1] + arrived[first + 1]], axis=0
            ).astype(BF16)
        axis_start("group", outgoing.at[0], slots, sem_id)

    def units_node_start(outgoing, group_slots, node_slots, sem_id):
        total = axis_finish("group", outgoing.at[0], group_slots, sem_id)
        outgoing[1] = total.astype(BF16)
        axis_start("node", outgoing.at[1], node_slots, sem_id + 1)

    def units_share(outgoing, node_slots, result, sem_id, pair_id):
        total = axis_finish("node", outgoing.at[1], node_slots, sem_id)
        for index in range(2):
            first = seq * 4 + 2 * index
            result[first] = total[index, 0:RANK]
            result[first + 1] = total[index, RANK : 2 * RANK]
        half_units = result.at[pl.ds(seq * 4, 4)]
        copy = to_partner(half_units, half_units, pair_id)
        copy.start()
        return copy

    left_copy = units_pair_start(r.lefts, r.lefts_arrived, 2)

    r.grad_attended[...] = mm_nt(r.grad_branch[...], r.low_out[...]).astype(BF16)
    r.err_out[...] += mm_tn(r.attended[...], r.grad_branch[...])
    for part in range(hidden_lanes // chunk):
        lanes = slice(part * chunk, (part + 1) * chunk)
        r.err_red[lanes, :] += mm_tn(r.activated[:, lanes], r.upstream[...])
        r.err_exp[:, lanes] += mm_tn(r.hidden_two[...], r.grad_pre[:, lanes])
    units_group_start(left_copy, r.lefts, r.lefts_arrived, r.lefts_out, r.lefts_group, 0)

    def grad_copy(i):
        return to_partner(r.grad_sent.at[i], r.grad_arrived.at[i], 8 + i)

    @pl.loop(0, images)
    def _(i):
        base = pl.multiple_of(i * block, 16)
        at = pl.ds(base, block)
        specials = pl.ds(pl.multiple_of(base + special, 8), 2)
        for pair in range(pairs):
            lanes = slice(pair * pair_width, (pair + 1) * pair_width)
            value_lanes = slice(width + pair * pair_width, width + (pair + 1) * pair_width)
            grad_mixed = stacked(r.grad_attended[at, lanes])
            query = stacked(r.query[at, lanes])
            probs = r.probs[i * pairs + pair]
            grad_probs = mm_nt(of_both(i, value_lanes), grad_mixed)
            delta = jnp.sum(probs * grad_probs, axis=0, keepdims=True)
            grad_scores = (probs * (grad_probs - delta)).astype(BF16)
            r.grad_query[at, lanes] = unstacked(mm_tn(grad_scores, of_both(i, lanes))) * (
                1.0 / math.sqrt(HEAD_DIM)
            )
            grad_keys = mm(grad_scores, query)
            grad_values = mm(probs.astype(BF16), grad_mixed)
            r.grad_own[i, :, lanes] = grad_keys[0:KEYS]
            r.grad_own[i, :, value_lanes] = grad_values[0:KEYS]
            r.grad_sent[i, :, lanes] = grad_keys[KEYS : 2 * KEYS]
            r.grad_sent[i, :, value_lanes] = grad_values[KEYS : 2 * KEYS]
        r.grad_sent[i, special : special + 2, :] = r.grad_own[i, special : special + 2, :]
        r.grad_sent[i, block : block + 2, 0:width] = r.grad_query[specials, :]
        grad_copy(i).start()

    units_node_start(r.lefts_out, r.lefts_group, r.lefts_node, 0)

    row_ids = lax.broadcasted_iota(jnp.int32, (block, 1), 0)
    halved = jnp.where((row_ids >= special) & (row_ids < special + 2), 0.5, 1.0)

    @pl.loop(0, images)
    def _(i):
        grad_copy(i).wait()
        base = pl.multiple_of(i * block, 16)
        at = pl.ds(base, block)
        specials = pl.ds(pl.multiple_of(base + special, 8), 2)
        r.grad_query[specials, :] += r.grad_arrived[i, block : block + 2, 0:width]
        query_part = r.grad_query[at, :].astype(BF16).astype(F32) * halved
        r.grad_qkv[at, 0:width] = query_part.astype(BF16)
        rest = (r.grad_own[i, 0:block, :] + r.grad_arrived[i, 0:block, :]).astype(BF16)
        r.grad_qkv[at, width : 3 * width] = (rest.astype(F32) * halved).astype(BF16)

    folded = mm_nt(r.new_f_in[...].astype(BF16), r.grad_qkv[...]).astype(BF16)
    r.left_in[...] += mm(folded, r.hidden_one[...])
    left_in_copy = to_partner(r.left_in, r.left_in_arrived, 4)
    left_in_copy.start()

    r.total[...] = mm_nt(r.grad_qkv[...], r.low_in[...])

    left_in_copy.wait()
    pair_sum = r.left_in[...] + r.left_in_arrived[...]
    r.left_in_out[...] = jnp.concatenate(
        [pair_sum[:, 0:256], jnp.concatenate([pair_sum[:, 256:384], jnp.zeros((RANK, 128), F32)], axis=1)],
        axis=0,
    ).astype(BF16)
    chips_start(r.left_in_out, r.left_in_slots, 5)

    left_share = units_share(r.lefts_out, r.lefts_node, r.lefts_total, 1, 3)
    r.gain_sum[...] = jnp.zeros_like(r.gain_sum)
    r.shift_sum[...] = jnp.zeros_like(r.shift_sum)

    @pl.loop(0, images)
    def _(i):
        at = pl.ds(pl.multiple_of(i * block, 16), block)
        back = normalise_back(i, small_row(0), r.xhat_one, r.scale_one, r.gain_sum, r.shift_sum)
        r.total[at, :] = (back + r.grad_middle[at, :]) * (2.0 - jnp.where(halved < 1.0, 0.0, 1.0))

    r.late_rows[...] = jnp.zeros_like(r.late_rows)
    r.late_rows[0:1, :] = r.gain_sum[...]
    r.late_rows[1:2, :] = r.shift_sum[...]
    r.late_rows[2:3, :] = mm(ones, r.grad_qkv[:, 0:width])[0:1]
    r.late_rows[3:4, :] = mm(ones, r.grad_qkv[:, 2 * width : 3 * width])[0:1]
    left_share.wait()
    inverse = 1.0 / workers
    basis_red = orthonormal(
        jnp.concatenate([r.lefts_total[part] for part in range(4)], axis=1) * inverse
    )
    basis_exp = orthonormal(r.lefts_total[4] * inverse)
    basis_out = orthonormal(r.lefts_total[5] * inverse)
    r.basis_red[...] = basis_red
    r.basis_exp[...] = basis_exp
    r.basis_out[...] = basis_out

    def right_of(basis, merged):
        both = jnp.concatenate([basis, basis - basis.astype(BF16).astype(F32)], axis=0).astype(BF16)
        product = mm(both, merged.astype(BF16))
        return product[0:RANK] + product[RANK : 2 * RANK]

    for part in range(4):
        lanes = slice(part * width, (part + 1) * width)
        r.rights[part] = right_of(basis_exp, r.err_exp[:, lanes])
    r.rights[4] = right_of(basis_red, r.err_red[...])
    r.rights[5] = right_of(basis_out, r.err_out[...])
    r.rights[6] = jnp.zeros((RANK, width), F32)
    r.rights[7] = jnp.zeros((RANK, width), F32)
    right_copy = units_pair_start(r.rights, r.rights_arrived, 5)

    for part in range(3):
        lanes = slice(part * width, (part + 1) * width)
        r.err_in[:, lanes] += mm_tn(r.hidden_one[...], r.grad_qkv[:, lanes])
    units_group_start(right_copy, r.rights, r.rights_arrived, r.rights_out, r.rights_group, 2)

    total = chips_finish(r.left_in_out, r.left_in_slots, 5)
    basis_in = orthonormal(
        jnp.concatenate([total[0:RANK], total[RANK : 2 * RANK, 0:128]], axis=1) * inverse
    )
    for part in range(3):
        lanes = slice(part * width, (part + 1) * width)
        r.right_in[part] = right_of(basis_in, r.err_in[:, lanes])
    r.right_in[3] = r.late_rows[...]
    right_in_copy = to_partner(r.right_in, r.right_in_arrived, 6)
    right_in_copy.start()
    for i in range(images):
        base = i * block
        r.mixed[:, i, :] = r.total[base : base + half, :] * r.mask_columns[i, 0:half, :]
        r.grad_special[i] = r.total[base + special : base + special + 2, :].astype(BF16)
    right_in_copy.wait()
    first = seq * 2
    r.right_in_out[...] = jnp.concatenate(
        [
            r.right_in[first] + r.right_in_arrived[first],
            r.right_in[first + 1] + r.right_in_arrived[first + 1],
        ],
        axis=0,
    ).astype(BF16)
    chips_start(r.right_in_out, r.right_in_slots, 4)
    units_node_start(r.rights_out, r.rights_group, r.rights_node, 2)
    r.grad_patch[...] = r.mixed[...].astype(BF16)

    def update(basis, right, error_ref, weight_ref, momentum_ref, lanes, row_start, row_count):
        left_stack, right_stack = outer_product(basis, right)
        at = slice(row_start, row_start + row_count)
        approx = mm_tn(left_stack, right_stack)
        error_ref[at, lanes] = error_ref[at, lanes] - approx
        momentum = DECAY * momentum_ref[at, lanes] + approx
        momentum_ref[at, lanes] = momentum
        weight_ref[at, lanes] = weight_ref[at, lanes] - RATE * momentum

    right_share = units_share(r.rights_out, r.rights_node, r.rights_total, 3, 7)
    loads["m_small"].wait()
    loads["m_in"].wait()
    loads["m_out"].wait()
    loads["m_exp"].wait()
    loads["m_red"].wait()
    right_share.wait()
    for part in range(4):
        lanes = slice(part * width, (part + 1) * width)
        right = r.rights_total[part] * inverse
        update(r.basis_exp[...], right, r.err_exp, r.new_exp, r.mom_exp, lanes, 0, width)
        r.new_f_exp[:, lanes] = right
        right = r.rights_total[4] * inverse
        update(
            r.basis_red[:, lanes],
            right,
            r.err_red,
            r.new_red,
            r.mom_red,
            slice(0, width),
            part * width,
            width,
        )
    r.new_f_red[...] = r.rights_total[4] * inverse
    right = r.rights_total[5] * inverse
    update(r.basis_out[...], right, r.err_out, r.new_out, r.mom_out, slice(0, width), 0, width)
    r.new_f_out[...] = right

    total = chips_finish(r.right_in_out, r.right_in_slots, 4)
    r.right_in_total[first] = total[0:RANK]
    r.right_in_total[first + 1] = total[RANK : 2 * RANK]
    half_units = r.right_in_total.at[pl.ds(first, 2)]
    share = to_partner(half_units, half_units, 12)
    share.start()
    share.wait()
    for part in range(3):
        lanes = slice(part * width, (part + 1) * width)
        right = r.right_in_total[part] * inverse
        update(basis_in, right, r.err_in, r.new_in, r.mom_in, lanes, 0, width)
        r.new_f_in[:, lanes] = right

    def small_update(at, grad):
        momentum = DECAY * r.mom_small[at, :] + grad * inverse
        r.mom_small[at, :] = momentum
        r.new_small[at, :] = r.new_small[at, :] - RATE * momentum

    small_update(slice(0, 4), r.right_in_total[3][0:4])
    small_update(slice(4, 12), r.lefts_total[6])


def store_kernel(count, *refs):
    sources, targets, sem = refs[:count], refs[count : 2 * count], refs[2 * count]
    copies = []
    for index in range(count):
        source, target = sources[index], targets[index]
        if len(source.shape) != len(target.shape):
            target = target.at[0]
        copies.append(pltpu.make_async_copy(source, target, sem.at[index]))
    for copy in copies:
        copy.start()
    for copy in copies:
        copy.wait()


def body(chips, groups, *args):
    args = list(args)
    for index in (0, 2):
        args[index] = jnp.transpose(args[index], (1, 0, 2))
    half, images, width = args[0].shape
    wide = args[8].shape[1]
    special = round_up(half, 8)
    block = round_up(special + 2, 16)
    rows = images * block
    out_shapes = [((half, images, width), BF16), ((images, 2, width), BF16)] * 2
    weight_shapes = [(width, 3 * width), (width, width), (width, wide), (wide, width)]
    small_shape = (args[10].shape, F32)
    out_shapes += [(shape, F32) for shape in weight_shapes] + [small_shape]
    out_shapes += [(shape, F32) for shape in weight_shapes] + [small_shape]
    out_shapes += [(shape, F32) for shape in weight_shapes]
    out_shapes += [((RANK, size), F32) for size in (3 * width, width, wide, width)]
    unit = (RANK, width)
    scratch = dict(
        raw_patch=pltpu.VMEM((half, images, width), BF16),
        raw_special=pltpu.VMEM((images, 2, width), BF16),
        raw_up=pltpu.VMEM((half, images, width), BF16),
        raw_special_up=pltpu.VMEM((images, 2, width), BF16),
        mixed=pltpu.VMEM((half, images, width), F32),
        rank=pltpu.VMEM((images, half), jnp.int32),
        flags=pltpu.VMEM((8, KEYS), F32),
        other_flags=pltpu.VMEM((8, KEYS), F32),
        mask_columns=pltpu.VMEM((images, 2 * KEYS, 1), F32),
        tokens=pltpu.VMEM((rows, width), F32),
        xhat_one=pltpu.VMEM((rows, width), F32),
        xhat_two=pltpu.VMEM((rows, width), F32),
        scale_one=pltpu.VMEM((rows, 1), F32),
        scale_two=pltpu.VMEM((rows, 1), F32),
        hidden_one=pltpu.VMEM((rows, width), BF16),
        hidden_two=pltpu.VMEM((rows, width), BF16),
        low_in=pltpu.VMEM((width, 3 * width), BF16),
        low_out=pltpu.VMEM((width, width), BF16),
        low_exp=pltpu.VMEM((width, wide), BF16),
        low_red=pltpu.VMEM((wide, width), BF16),
        query=pltpu.VMEM((rows, width), BF16),
        keys=pltpu.VMEM((2, images, KEYS, 2 * width), BF16),
        upstream=pltpu.VMEM((rows, width), BF16),
        probs=pltpu.VMEM((images * HEADS // 2, 2 * KEYS, 2 * block), F32),
        attended=pltpu.VMEM((rows, width), BF16),
        middle=pltpu.VMEM((rows, width), F32),
        wide=pltpu.VMEM((rows, 2 * width), F32),
        activated=pltpu.VMEM((rows, wide), BF16),
        slope=pltpu.VMEM((rows, wide), F32),
        grad_pre=pltpu.VMEM((rows, wide), BF16),
        total=pltpu.VMEM((rows, width), F32),
        gain_sum=pltpu.VMEM((1, width), F32),
        shift_sum=pltpu.VMEM((1, width), F32),
        grad_middle=pltpu.VMEM((rows, width), F32),
        grad_branch=pltpu.VMEM((rows, width), BF16),
        grad_attended=pltpu.VMEM((rows, width), BF16),
        grad_query=pltpu.VMEM((rows, width), F32),
        grad_own=pltpu.VMEM((images, KEYS, 2 * width), F32),
        grad_sent=pltpu.VMEM((images, KEYS, 2 * width), F32),
        grad_arrived=pltpu.VMEM((images, KEYS, 2 * width), F32),
        grad_qkv=pltpu.VMEM((rows, 3 * width), BF16),
        lefts=pltpu.VMEM((8,) + unit, F32),
        lefts_arrived=pltpu.VMEM((8,) + unit, F32),
        lefts_out=pltpu.VMEM((2, 2, 2 * RANK, width), BF16),
        lefts_group=pltpu.VMEM((groups, 2, 2 * RANK, width), BF16),
        lefts_node=pltpu.VMEM((chips // groups, 2, 2 * RANK, width), BF16),
        lefts_total=pltpu.VMEM((8,) + unit, F32),
        rights=pltpu.VMEM((8,) + unit, F32),
        rights_arrived=pltpu.VMEM((8,) + unit, F32),
        rights_out=pltpu.VMEM((2, 2, 2 * RANK, width), BF16),
        rights_group=pltpu.VMEM((groups, 2, 2 * RANK, width), BF16),
        rights_node=pltpu.VMEM((chips // groups, 2, 2 * RANK, width), BF16),
        rights_total=pltpu.VMEM((8,) + unit, F32),
        left_in=pltpu.VMEM(unit, F32),
        left_in_arrived=pltpu.VMEM(unit, F32),
        left_in_out=pltpu.VMEM((2 * RANK, 256), BF16),
        left_in_slots=pltpu.VMEM((chips, 2 * RANK, 256), BF16),
        right_in=pltpu.VMEM((4,) + unit, F32),
        right_in_arrived=pltpu.VMEM((4,) + unit, F32),
        right_in_out=pltpu.VMEM((2 * RANK, width), BF16),
        right_in_slots=pltpu.VMEM((chips, 2 * RANK, width), BF16),
        right_in_total=pltpu.VMEM((4,) + unit, F32),
        basis_red=pltpu.VMEM((RANK, wide), F32),
        basis_exp=pltpu.VMEM(unit, F32),
        basis_out=pltpu.VMEM(unit, F32),
        late_rows=pltpu.VMEM(unit, F32),
        load_sem=pltpu.SemaphoreType.DMA((23,)),
        pair_send=pltpu.SemaphoreType.DMA((13,)),
        pair_recv=pltpu.SemaphoreType.DMA((13,)),
        chip_send=pltpu.SemaphoreType.DMA((6, chips)),
        chip_recv=pltpu.SemaphoreType.DMA((6, chips)),
    )
    names = INPUTS + OUTPUTS + tuple(scratch)
    in_specs = [
        pl.BlockSpec(memory_space=pltpu.SMEM if name == "keep_count" else pl.ANY)
        for name in INPUTS
    ]
    in_vmem = pl.BlockSpec(memory_space=pltpu.VMEM)
    results = pl.pallas_call(
        functools.partial(layer_kernel, chips, groups, images, half, names),
        out_shape=[pltpu.VMEM(shape, dtype) for shape, dtype in out_shapes],
        in_specs=in_specs,
        out_specs=[in_vmem] * len(OUTPUTS),
        scratch_shapes=list(scratch.values()),
        compiler_params=pltpu.CompilerParams(
            collective_id=0, has_side_effects=True, vmem_limit_bytes=40 << 20
        ),
        name="layer",
    )(*args[:20], *[jnp.transpose(factor) for factor in args[20:]])
    final_shapes = [
        jax.ShapeDtypeStruct((1,) + shape if 14 <= index < 18 else shape, dtype)
        for index, (shape, dtype) in enumerate(out_shapes)
    ]
    count = len(OUTPUTS)
    stored = list(
        pl.pallas_call(
            functools.partial(store_kernel, count),
            out_shape=final_shapes,
            in_specs=[in_vmem] * count,
            out_specs=[pl.BlockSpec(memory_space=pl.ANY)] * count,
            scratch_shapes=[pltpu.SemaphoreType.DMA((count,))],
            compiler_params=pltpu.CompilerParams(vmem_limit_bytes=1 << 20),
            name="store",
        )(*results)
    )
    for index in (0, 2):
        stored[index] = jnp.transpose(stored[index], (1, 0, 2))
    return (*stored[:18], *[jnp.transpose(factor) for factor in stored[18:]])


def solution(mesh):
    images_over = ("node", "group")
    rows_spec = P(images_over, "seq", None)
    special_spec = P(images_over, None, None)
    worker_spec = P(("seq", "node", "group"), None, None)
    whole = P()
    placed = (
        (rows_spec, special_spec) * 2
        + (P(images_over, "seq"), P(images_over))
        + (whole,) * 10
        + (worker_spec,) * 4
        + (whole,) * 4
    )
    groups = mesh.shape["group"]
    chips = mesh.shape["node"] * groups
    return jax.shard_map(
        functools.partial(body, chips, groups),
        mesh=mesh,
        in_specs=placed,
        out_specs=(rows_spec, special_spec) * 2
        + (whole,) * 10
        + (worker_spec,) * 4
        + (whole,) * 4,
        check_vma=False,
    )
```

time: 561 us -> 60.5 us (0.11); the launches traced: 552 us -> 60.4 us
  other arithmetic: 249 us -> 0 us
  waiting for transfers between devices: 83.7 us -> 0 us
  matrix products: 75.3 us -> 0 us
  Pallas kernels: 0 us -> 59.5 us
  blocking collectives: 59.4 us -> 0 us
  local copies, waits for them, and re-layouts: 47.5 us -> 0 us
  between operations: 36.8 us -> 0.84 us
    reduce_sum x65 -> x0, other arithmetic: 154 us -> none  [the longest x39 117 us: orthonormal(): column = column - jnp.sum(earlier * column) * earlier]
    psum x2 -> x0, waiting for transfers between devices: 83.7 us -> none  [the longest x1 49.5 us: body(): lax.psum((left_parts[0], left_parts[1], left_parts[2], left_parts[3], gra...]
    dot_general x30 -> x0, matrix products: 75.3 us -> none  [the longest x4 21.1 us: body(): approx = jnp.dot(basis_list[which], right_mean.T, precision=HIGH)]
    mul x8 -> x0, other arithmetic: 73.6 us -> none  [the longest x7 71.1 us: orthonormal(): columns.append(column * lax.rsqrt(jnp.sum(column * column) + EPSILON))]
    pallas_call x0 -> x2, Pallas kernels: none -> 59.5 us  [the longest x1 51.9 us: body(): pl.pallas_call(functools.partial(layer_kernel, chips, groups, images, hal...]
    psum x3 -> x0, blocking collectives: 59.4 us -> none  [the longest x1 28 us: body(): lax.psum(right_parts[0].astype(jnp.bfloat16), ('seq', 'node'))]
    reshape x12 -> x0, local copies, waits for them, and re-layouts: 25.8 us -> none  [the longest x1 13.1 us: body(): jnp.concatenate([special_low, patch_qkv], axis=1)]
    unnamed x119 -> x0, local copies, waits for them, and re-layouts: 7.88 us -> none
  transfers between devices with their start and end apart: 5 -> 0, of which waited for: 2 -> 0; matrix products, arithmetic and copies ran while one was open for 8% -> 0% of each run, Pallas kernels for 0% -> 0%
where the time goes in v1:
time: 60.5 us; the launch traced here: 60.4 us
  Pallas kernels  59.5 us (98%)
  between operations  0.84 us (1%)
    pallas_call x1, Pallas kernels, body(): pl.pallas_call(functools.partial(layer_kernel, chips, groups, images, hal...  51.9 us
    pallas_call x1, Pallas kernels, body(): pl.pallas_call(functools.partial(store_kernel, count), out_shape=final_sh...  7.67 us

profile of v1, /device:TPU:0, one launch (start us, length us, event | category | flops | bytes accessed | tf_op | source)
XLA Modules:
  0.0 60.4 jit_solution(7263245696523627331)
XLA Ops:
  0.7 51.9 %layer.1 = (bf16[98,4,384]{2,1,0:T(4,128)(2,1)S(1)}, bf16[4,2,384]{2,1,0:T(2,128)(2,1)S(1)}, bf16[98,4,384]{2,1,0:T(4,128)(2,1)S(1)}, bf16[4,2,384]{2,1,0:T(2,12...) custom-call(bf16[98,4,384]{2,1,0:T(4,128)(2,1)} %bitcast.12, ...), custom_call_target="tpu_custom_call" | custom-call | tf_op jit(solution)/shard_map/layer/pallas_call | solution.py:844
  52.6 7.7 %store.1 = (bf16[98,4,384]{2,1,0:T(4,128)(2,1)}, bf16[4,2,384]{2,1,0:T(2,128)(2,1)}, bf16[98,4,384]{2,1,0:T(4,128)(2,1)}, bf16[4,2,384]{2,1,0:T(2,128)(2,1)}, f3...) custom-call(bf16[98,4,384]{2,1,0:T(4,128)(2,1)S(1)} %get-tuple-eleme, ...), custom_call_target="tpu_custom_call" | custom-call | tf_op jit(solution)/shard_map/store/pallas_call | solution.py:861

commit v2 on v1

--- a/solution.py
+++ b/solution.py
@@ -67,6 +67,9 @@
     "new_f_exp",
     "new_f_red",
 )
+BASES = ("basis_in", "basis_out", "basis_exp", "basis_red")
+KINDS = ("new_", "mom_", "err_")
+MATRICES = ("in", "out", "exp", "red")
 KEYS = 128
 
 
@@ -148,26 +151,33 @@
     load("tokens", r.patch_tokens, r.raw_patch)
     load("special", r.special_tokens, r.raw_special)
     load("rank", r.patch_rank, r.rank)
+    load("count", r.keep_count, r.count)
     load("small", r.small_params, r.new_small)
     load("w_in", r.project_in, r.new_in)
-    load("f_in", r.project_in_factor, r.new_f_in)
-    load("f_out", r.project_out_factor, r.new_f_out)
-    load("f_exp", r.expand_factor, r.new_f_exp)
-    load("f_red", r.reduce_factor, r.new_f_red)
-    load("upstream", r.patch_upstream, r.raw_up)
-    load("special_up", r.special_upstream, r.raw_special_up)
-    load("e_in", r.project_in_error.at[0], r.err_in)
-    load("e_exp", r.expand_error.at[0], r.err_exp)
-    load("e_red", r.reduce_error.at[0], r.err_red)
-    load("e_out", r.project_out_error.at[0], r.err_out)
-    load("w_out", r.project_out, r.new_out)
-    load("w_exp", r.expand_weight, r.new_exp)
-    load("w_red", r.reduce_weight, r.new_red)
-    load("m_small", r.small_momentum, r.mom_small)
-    load("m_out", r.project_out_momentum, r.mom_out)
-    load("m_exp", r.expand_momentum, r.mom_exp)
-    load("m_red", r.reduce_momentum, r.mom_red)
-    load("m_in", r.project_in_momentum, r.mom_in)
+
+    def load_second():
+        load("upstream", r.patch_upstream, r.raw_up)
+        load("special_up", r.special_upstream, r.raw_special_up)
+        load("f_in", r.project_in_factor, r.new_f_in)
+        load("f_out", r.project_out_factor, r.new_f_out)
+        load("f_exp", r.expand_factor, r.new_f_exp)
+        load("f_red", r.reduce_factor, r.new_f_red)
+        load("e_in", r.project_in_error.at[0], r.err_in)
+        load("e_exp", r.expand_error.at[0], r.err_exp)
+        load("e_red", r.reduce_error.at[0], r.err_red)
+        load("e_out", r.project_out_error.at[0], r.err_out)
+
+    def load_third():
+        load("w_out", r.project_out, r.new_out)
+        load("w_exp", r.expand_weight, r.new_exp)
+        load("w_red", r.reduce_weight, r.new_red)
+
+    def load_last():
+        load("m_small", r.small_momentum, r.mom_small)
+        load("m_out", r.project_out_momentum, r.mom_out)
+        load("m_exp", r.expand_momentum, r.mom_exp)
+        load("m_red", r.reduce_momentum, r.mom_red)
+        load("m_in", r.project_in_momentum, r.mom_in)
 
     barrier = pltpu.get_barrier_semaphore()
     pl.semaphore_signal(barrier, inc=1, device_id={"seq": partner}, device_id_type=MESH)
@@ -267,10 +277,11 @@
         return total
 
     loads["rank"].wait()
+    loads["count"].wait()
     r.flags[...] = jnp.zeros_like(r.flags)
     for i in range(images):
         r.flags[i : i + 1, 0:half] = jnp.where(
-            r.rank[i : i + 1, :] < r.keep_count[i], 1.0, 0.0
+            r.rank[i : i + 1, :] < r.count[i], 1.0, 0.0
         ).astype(F32)
     lane_ids = lax.broadcasted_iota(jnp.int32, (1, KEYS), 1)
     special_lanes = jnp.where((lane_ids >= special) & (lane_ids < special + 2), 1.0, 0.0)
@@ -313,11 +324,12 @@
         normalise(r.tokens, i, small_row(0), small_row(1), r.xhat_one, r.scale_one, r.hidden_one)
 
     loads["w_in"].wait()
-    r.low_in[...] = r.new_in[...].astype(BF16)
+    load_second()
+    r.low_in[0:width, :] = r.new_in[...].astype(BF16)
     for i in range(images):
         r.keys[0, i, block:KEYS, :] = jnp.zeros((KEYS - block, 2 * width), BF16)
     for part in (1, 2, 0):
-        product = mm(r.hidden_one[...], r.low_in[:, part * width : (part + 1) * width])
+        product = mm(r.hidden_one[...], r.low_in[0:width, part * width : (part + 1) * width])
         if part == 0:
             query = (product + small_row(2)).astype(BF16).astype(F32) * (
                 1.0 / math.sqrt(HEAD_DIM)
@@ -352,15 +364,29 @@
         )
         r.middle[base : base + half, :] = r.mixed[:, i, :]
         r.middle[base + special : base + special + 2, :] = 0.5 * r.raw_special_up[i].astype(F32)
+    r.lefts[6, 3:4, :] = jnp.sum(r.middle[...], axis=0, keepdims=True)
     r.upstream[...] = r.middle[...].astype(BF16)
     loads["f_in"].wait()
     loads["f_out"].wait()
     loads["f_exp"].wait()
     loads["f_red"].wait()
+
+    def with_factor(low_ref, factor_ref):
+        factor = factor_ref[...]
+        low_ref[width : width + 2 * RANK, :] = jnp.concatenate(
+            [factor, jnp.zeros_like(factor)], axis=0
+        ).astype(BF16)
+
+    with_factor(r.low_in, r.new_f_in)
+    with_factor(r.low_out, r.new_f_out)
+    with_factor(r.low_exp, r.new_f_exp)
+    folded_red = mm_nt(r.new_f_red[...].astype(BF16), r.upstream[...])
+    r.folded_red[...] = folded_red.astype(BF16)
     loads["e_in"].wait()
     r.left_in[...] = error_left(r.err_in, r.new_f_in, 0, width)
     loads["e_exp"].wait()
     r.lefts[4] = error_left(r.err_exp, r.new_f_exp, 0, width)
+    load_third()
     loads["e_red"].wait()
     for part in range(4):
         r.lefts[part] = error_left(r.err_red, r.new_f_red, part * width, width)
@@ -393,21 +419,28 @@
     def _(i):
         at = pl.ds(pl.multiple_of(i * block, 16), block)
         valid = r.mask_columns[i] > 0.5
+
+        def lanes_of(pair, first=0):
+            return slice(first + pair * pair_width, first + (pair + 1) * pair_width)
+
         for pair in range(pairs):
-            lanes = slice(pair * pair_width, (pair + 1) * pair_width)
-            value_lanes = slice(width + pair * pair_width, width + (pair + 1) * pair_width)
-            scores = mm_nt(of_both(i, lanes), stacked(r.query[at, lanes]))
-            scores = jnp.where(valid, scores, -1e30)
+            scores = mm_nt(of_both(i, lanes_of(pair)), stacked(r.query[at, lanes_of(pair)]))
+            r.probs[i * pairs + pair] = jnp.where(valid, scores, -1e30)
+        for pair in range(pairs):
+            scores = r.probs[i * pairs + pair]
             top = jnp.max(scores, axis=0, keepdims=True)
             weights = jnp.exp(scores - top)
             probs = weights * (1.0 / jnp.sum(weights, axis=0, keepdims=True))
             r.probs[i * pairs + pair] = probs
-            mixed = mm_tn(probs.astype(BF16), of_both(i, value_lanes))
-            r.attended[at, lanes] = unstacked(mixed).astype(BF16)
+            r.low_probs[pair] = probs.astype(BF16)
+        for pair in range(pairs):
+            mixed = mm_tn(r.low_probs[pair], of_both(i, lanes_of(pair, width)))
+            r.attended[at, lanes_of(pair)] = unstacked(mixed).astype(BF16)
 
     loads["w_out"].wait()
-    r.low_out[...] = r.new_out[...].astype(BF16)
-    r.middle[...] = r.tokens[...] + mm(r.attended[...], r.low_out[...]) + small_row(4)
+    load_last()
+    r.low_out[0:width, :] = r.new_out[...].astype(BF16)
+    r.middle[...] = r.tokens[...] + mm(r.attended[...], r.low_out[0:width, :]) + small_row(4)
 
     @pl.loop(0, images)
     def _(i):
@@ -417,7 +450,7 @@
     chunk = 2 * width
     hidden_lanes = r.low_exp.shape[1]
     loads["w_exp"].wait()
-    r.low_exp[...] = r.new_exp[...].astype(BF16)
+    r.low_exp[0:width, :] = r.new_exp[...].astype(BF16)
     loads["w_red"].wait()
     r.low_red[...] = r.new_red[...].astype(BF16)
     bias_rows = chunk // width
@@ -427,7 +460,7 @@
         bias = jnp.concatenate(
             [small_row(8 + part * bias_rows + index) for index in range(bias_rows)], axis=1
         )
-        r.wide[...] = mm(r.hidden_two[...], r.low_exp[:, lanes])
+        r.wide[...] = mm(r.hidden_two[...], r.low_exp[0:width, lanes])
 
         @pl.loop(0, rows_all // strip)
         def _(index):
@@ -446,11 +479,9 @@
 
     r.out_patch[...] = r.mixed[...].astype(BF16)
 
-    folded = mm_nt(r.new_f_red[...].astype(BF16), r.upstream[...]).astype(BF16)
     for part in range(4):
         lanes = slice(part * width, (part + 1) * width)
-        r.lefts[part] += mm(folded, r.activated[:, lanes])
-    ones = jnp.ones((8, rows_all), BF16)
+        r.lefts[part] += mm(r.folded_red[...], r.activated[:, lanes])
     for part in range(hidden_lanes // chunk):
         lanes = slice(part * chunk, (part + 1) * chunk)
         grad_act = mm_nt(r.upstream[...], r.low_red[lanes, :]).astype(BF16).astype(F32)
@@ -462,11 +493,16 @@
             r.lefts[6, first : first + 1, :] = row[:, index * width : (index + 1) * width]
         back = mm_nt(r.grad_pre[:, lanes], r.low_exp[:, lanes])
         if part == 0:
-            r.total[...] = back
+            r.total[...] = back[:, 0:width]
+            r.folded[...] = back[:, width : width + 2 * RANK]
         else:
-            r.total[...] += back
-    folded = mm_nt(r.new_f_exp[...].astype(BF16), r.grad_pre[...]).astype(BF16)
-    r.lefts[4] += mm(folded, r.hidden_two[...])
+            r.total[...] += back[:, 0:width]
+            r.folded[...] += back[:, width : width + 2 * RANK]
+
+    def left_of(hidden_ref):
+        return mm_tn(r.folded[...].astype(BF16), hidden_ref[...])[0:RANK]
+
+    r.lefts[4] += left_of(r.hidden_two)
 
     def normalise_back(i, gain, xhat_ref, scale_ref, gain_ref, shift_ref):
         at = pl.ds(pl.multiple_of(i * block, 16), block)
@@ -481,6 +517,7 @@
 
     r.gain_sum[...] = jnp.zeros_like(r.gain_sum)
     r.shift_sum[...] = jnp.zeros_like(r.shift_sum)
+    r.branch_sum[...] = jnp.zeros_like(r.branch_sum)
 
     @pl.loop(0, images)
     def _(i):
@@ -488,15 +525,18 @@
         back = normalise_back(i, small_row(5), r.xhat_two, r.scale_two, r.gain_sum, r.shift_sum)
         grad = r.upstream[at, :].astype(F32) + back
         r.grad_middle[at, :] = grad
-        r.grad_branch[at, :] = grad.astype(BF16)
+        low = grad.astype(BF16)
+        r.grad_branch[at, :] = low
+        r.branch_sum[...] += jnp.sum(low.astype(F32), axis=0, keepdims=True)
 
     r.lefts[6, 1:2, :] = r.gain_sum[...]
     r.lefts[6, 2:3, :] = r.shift_sum[...]
-    r.lefts[6, 3:4, :] = mm(ones, r.upstream[...])[0:1]
-    r.lefts[6, 0:1, :] = mm(ones, r.grad_branch[...])[0:1]
+    r.lefts[6, 0:1, :] = r.branch_sum[...]
     r.lefts[7] = jnp.zeros((RANK, width), F32)
-    folded = mm_nt(r.new_f_out[...].astype(BF16), r.grad_branch[...]).astype(BF16)
-    r.lefts[5] += mm(folded, r.attended[...])
+    back = mm_nt(r.grad_branch[...], r.low_out[...])
+    r.grad_attended[...] = back[:, 0:width].astype(BF16)
+    r.folded[...] = back[:, width : width + 2 * RANK]
+    r.lefts[5] += left_of(r.attended)
 
     def units_pair_start(units, arrived, sem_id):
         copy = to_partner(units, arrived, sem_id)
@@ -530,14 +570,6 @@
 
     left_copy = units_pair_start(r.lefts, r.lefts_arrived, 2)
 
-    r.grad_attended[...] = mm_nt(r.grad_branch[...], r.low_out[...]).astype(BF16)
-    r.err_out[...] += mm_tn(r.attended[...], r.grad_branch[...])
-    for part in range(hidden_lanes // chunk):
-        lanes = slice(part * chunk, (part + 1) * chunk)
-        r.err_red[lanes, :] += mm_tn(r.activated[:, lanes], r.upstream[...])
-        r.err_exp[:, lanes] += mm_tn(r.hidden_two[...], r.grad_pre[:, lanes])
-    units_group_start(left_copy, r.lefts, r.lefts_arrived, r.lefts_out, r.lefts_group, 0)
-
     def grad_copy(i):
         return to_partner(r.grad_sent.at[i], r.grad_arrived.at[i], 8 + i)
 
@@ -546,32 +578,44 @@
         base = pl.multiple_of(i * block, 16)
         at = pl.ds(base, block)
         specials = pl.ds(pl.multiple_of(base + special, 8), 2)
+
+        def lanes_of(pair, first=0):
+            return slice(first + pair * pair_width, first + (pair + 1) * pair_width)
+
         for pair in range(pairs):
-            lanes = slice(pair * pair_width, (pair + 1) * pair_width)
-            value_lanes = slice(width + pair * pair_width, width + (pair + 1) * pair_width)
-            grad_mixed = stacked(r.grad_attended[at, lanes])
-            query = stacked(r.query[at, lanes])
+            grad_mixed = stacked(r.grad_attended[at, lanes_of(pair)])
+            r.grad_probs[pair] = mm_nt(of_both(i, lanes_of(pair, width)), grad_mixed)
+        for pair in range(pairs):
             probs = r.probs[i * pairs + pair]
-            grad_probs = mm_nt(of_both(i, value_lanes), grad_mixed)
-            delta = jnp.sum(probs * grad_probs, axis=0, keepdims=True)
-            grad_scores = (probs * (grad_probs - delta)).astype(BF16)
-            r.grad_query[at, lanes] = unstacked(mm_tn(grad_scores, of_both(i, lanes))) * (
-                1.0 / math.sqrt(HEAD_DIM)
-            )
-            grad_keys = mm(grad_scores, query)
-            grad_values = mm(probs.astype(BF16), grad_mixed)
-            r.grad_own[i, :, lanes] = grad_keys[0:KEYS]
-            r.grad_own[i, :, value_lanes] = grad_values[0:KEYS]
-            r.grad_sent[i, :, lanes] = grad_keys[KEYS : 2 * KEYS]
-            r.grad_sent[i, :, value_lanes] = grad_values[KEYS : 2 * KEYS]
+            weighted = probs * r.grad_probs[pair]
+            delta = jnp.sum(weighted, axis=0, keepdims=True)
+            r.low_probs[pair] = (weighted - probs * delta).astype(BF16)
+        for pair in range(pairs):
+            grad_scores = r.low_probs[pair]
+            r.grad_query[at, lanes_of(pair)] = unstacked(
+                mm_tn(grad_scores, of_both(i, lanes_of(pair)))
+            ) * (1.0 / math.sqrt(HEAD_DIM))
+            grad_keys = mm(grad_scores, stacked(r.query[at, lanes_of(pair)]))
+            r.grad_own[i, :, lanes_of(pair)] = grad_keys[0:KEYS]
+            r.grad_sent[i, :, lanes_of(pair)] = grad_keys[KEYS : 2 * KEYS]
+        for pair in range(pairs):
+            grad_mixed = stacked(r.grad_attended[at, lanes_of(pair)])
+            grad_values = mm(r.probs[i * pairs + pair].astype(BF16), grad_mixed)
+            r.grad_own[i, :, lanes_of(pair, width)] = grad_values[0:KEYS]
+            r.grad_sent[i, :, lanes_of(pair, width)] = grad_values[KEYS : 2 * KEYS]
         r.grad_sent[i, special : special + 2, :] = r.grad_own[i, special : special + 2, :]
         r.grad_sent[i, block : block + 2, 0:width] = r.grad_query[specials, :]
         grad_copy(i).start()
 
+        @pl.when(i == 0)
+        def _():
+            units_group_start(left_copy, r.lefts, r.lefts_arrived, r.lefts_out, r.lefts_group, 0)
+
     units_node_start(r.lefts_out, r.lefts_group, r.lefts_node, 0)
 
     row_ids = lax.broadcasted_iota(jnp.int32, (block, 1), 0)
     halved = jnp.where((row_ids >= special) & (row_ids < special + 2), 0.5, 1.0)
+    r.late_rows[...] = jnp.zeros_like(r.late_rows)
 
     @pl.loop(0, images)
     def _(i):
@@ -582,15 +626,18 @@
         r.grad_query[specials, :] += r.grad_arrived[i, block : block + 2, 0:width]
         query_part = r.grad_query[at, :].astype(BF16).astype(F32) * halved
         r.grad_qkv[at, 0:width] = query_part.astype(BF16)
+        r.late_rows[2:3, :] += jnp.sum(query_part, axis=0, keepdims=True)
         rest = (r.grad_own[i, 0:block, :] + r.grad_arrived[i, 0:block, :]).astype(BF16)
-        r.grad_qkv[at, width : 3 * width] = (rest.astype(F32) * halved).astype(BF16)
-
-    folded = mm_nt(r.new_f_in[...].astype(BF16), r.grad_qkv[...]).astype(BF16)
-    r.left_in[...] += mm(folded, r.hidden_one[...])
+        rest = rest.astype(F32) * halved
+        r.late_rows[3:4, :] += jnp.sum(rest[:, width : 2 * width], axis=0, keepdims=True)
+        r.grad_qkv[at, width : 3 * width] = rest.astype(BF16)
+
+    back = mm_nt(r.grad_qkv[...], r.low_in[...])
+    r.total[...] = back[:, 0:width]
+    r.folded[...] = back[:, width : width + 2 * RANK]
+    r.left_in[...] += left_of(r.hidden_one)
     left_in_copy = to_partner(r.left_in, r.left_in_arrived, 4)
     left_in_copy.start()
-
-    r.total[...] = mm_nt(r.grad_qkv[...], r.low_in[...])
 
     left_in_copy.wait()
     pair_sum = r.left_in[...] + r.left_in_arrived[...]
@@ -600,6 +647,11 @@
     ).astype(BF16)
     chips_start(r.left_in_out, r.left_in_slots, 5)
 
+    r.err_out[...] += mm_tn(r.attended[...], r.grad_branch[...])
+    for part in range(hidden_lanes // chunk):
+        lanes = slice(part * chunk, (part + 1) * chunk)
+        r.err_red[lanes, :] += mm_tn(r.activated[:, lanes], r.upstream[...])
+        r.err_exp[:, lanes] += mm_tn(r.hidden_two[...], r.grad_pre[:, lanes])
     left_share = units_share(r.lefts_out, r.lefts_node, r.lefts_total, 1, 3)
     r.gain_sum[...] = jnp.zeros_like(r.gain_sum)
     r.shift_sum[...] = jnp.zeros_like(r.shift_sum)
@@ -608,13 +660,10 @@
     def _(i):
         at = pl.ds(pl.multiple_of(i * block, 16), block)
         back = normalise_back(i, small_row(0), r.xhat_one, r.scale_one, r.gain_sum, r.shift_sum)
-        r.total[at, :] = (back + r.grad_middle[at, :]) * (2.0 - jnp.where(halved < 1.0, 0.0, 1.0))
-
-    r.late_rows[...] = jnp.zeros_like(r.late_rows)
+        r.total[at, :] = (back + r.grad_middle[at, :]) * jnp.where(halved < 1.0, 2.0, 1.0)
+
     r.late_rows[0:1, :] = r.gain_sum[...]
     r.late_rows[1:2, :] = r.shift_sum[...]
-    r.late_rows[2:3, :] = mm(ones, r.grad_qkv[:, 0:width])[0:1]
-    r.late_rows[3:4, :] = mm(ones, r.grad_qkv[:, 2 * width : 3 * width])[0:1]
     left_share.wait()
     inverse = 1.0 / workers
     basis_red = orthonormal(
@@ -639,7 +688,6 @@
     r.rights[6] = jnp.zeros((RANK, width), F32)
     r.rights[7] = jnp.zeros((RANK, width), F32)
     right_copy = units_pair_start(r.rights, r.rights_arrived, 5)
-
     for part in range(3):
         lanes = slice(part * width, (part + 1) * width)
         r.err_in[:, lanes] += mm_tn(r.hidden_one[...], r.grad_qkv[:, lanes])
@@ -649,6 +697,7 @@
     basis_in = orthonormal(
         jnp.concatenate([total[0:RANK], total[RANK : 2 * RANK, 0:128]], axis=1) * inverse
     )
+    r.basis_in[...] = basis_in
     for part in range(3):
         lanes = slice(part * width, (part + 1) * width)
         r.right_in[part] = right_of(basis_in, r.err_in[:, lanes])
@@ -672,42 +721,21 @@
     units_node_start(r.rights_out, r.rights_group, r.rights_node, 2)
     r.grad_patch[...] = r.mixed[...].astype(BF16)
 
-    def update(basis, right, error_ref, weight_ref, momentum_ref, lanes, row_start, row_count):
-        left_stack, right_stack = outer_product(basis, right)
-        at = slice(row_start, row_start + row_count)
-        approx = mm_tn(left_stack, right_stack)
-        error_ref[at, lanes] = error_ref[at, lanes] - approx
-        momentum = DECAY * momentum_ref[at, lanes] + approx
-        momentum_ref[at, lanes] = momentum
-        weight_ref[at, lanes] = weight_ref[at, lanes] - RATE * momentum
-
+    for name in ("m_small", "m_in", "m_out", "m_exp", "m_red"):
+        loads[name].wait()
     right_share = units_share(r.rights_out, r.rights_node, r.rights_total, 3, 7)
-    loads["m_small"].wait()
-    loads["m_in"].wait()
-    loads["m_out"].wait()
-    loads["m_exp"].wait()
-    loads["m_red"].wait()
     right_share.wait()
     for part in range(4):
-        lanes = slice(part * width, (part + 1) * width)
-        right = r.rights_total[part] * inverse
-        update(r.basis_exp[...], right, r.err_exp, r.new_exp, r.mom_exp, lanes, 0, width)
-        r.new_f_exp[:, lanes] = right
-        right = r.rights_total[4] * inverse
-        update(
-            r.basis_red[:, lanes],
-            right,
-            r.err_red,
-            r.new_red,
-            r.mom_red,
-            slice(0, width),
-            part * width,
-            width,
-        )
+        r.new_f_exp[:, part * width : (part + 1) * width] = r.rights_total[part] * inverse
     r.new_f_red[...] = r.rights_total[4] * inverse
-    right = r.rights_total[5] * inverse
-    update(r.basis_out[...], right, r.err_out, r.new_out, r.mom_out, slice(0, width), 0, width)
-    r.new_f_out[...] = right
+    r.new_f_out[...] = r.rights_total[5] * inverse
+
+    def small_update(at, grad):
+        momentum = DECAY * r.mom_small[at, :] + grad * inverse
+        r.mom_small[at, :] = momentum
+        r.new_small[at, :] = r.new_small[at, :] - RATE * momentum
+
+    small_update(slice(4, 12), r.lefts_total[6])
 
     total = chips_finish(r.right_in_out, r.right_in_slots, 4)
     r.right_in_total[first] = total[0:RANK]
@@ -717,30 +745,41 @@
     share.start()
     share.wait()
     for part in range(3):
-        lanes = slice(part * width, (part + 1) * width)
-        right = r.right_in_total[part] * inverse
-        update(basis_in, right, r.err_in, r.new_in, r.mom_in, lanes, 0, width)
-        r.new_f_in[:, lanes] = right
-
-    def small_update(at, grad):
-        momentum = DECAY * r.mom_small[at, :] + grad * inverse
-        r.mom_small[at, :] = momentum
-        r.new_small[at, :] = r.new_small[at, :] - RATE * momentum
-
+        r.new_f_in[:, part * width : (part + 1) * width] = r.right_in_total[part] * inverse
     small_update(slice(0, 4), r.right_in_total[3][0:4])
-    small_update(slice(4, 12), r.lefts_total[6])
-
-
-def store_kernel(count, *refs):
-    sources, targets, sem = refs[:count], refs[count : 2 * count], refs[2 * count]
+
+
+def store_kernel(names, targets, *all_refs):
+    refs = Names()
+    for name, ref in zip(names, all_refs):
+        setattr(refs, name, ref)
     copies = []
-    for index in range(count):
-        source, target = sources[index], targets[index]
-        if len(source.shape) != len(target.shape):
-            target = target.at[0]
-        copies.append(pltpu.make_async_copy(source, target, sem.at[index]))
-    for copy in copies:
-        copy.start()
+
+    def send(source, target):
+        copies.append(pltpu.make_async_copy(source, target, refs.sem.at[len(copies)]))
+        copies[-1].start()
+
+    updated = {kind + which for kind in KINDS for which in MATRICES}
+    for name in targets:
+        if name not in updated:
+            send(getattr(refs, name), getattr(refs, "hbm_" + name))
+    rows = 128
+    for which in ("exp", "red", "out", "in"):
+        weight, momentum, error = (getattr(refs, kind + which) for kind in KINDS)
+        new_weight, new_momentum, new_error = (getattr(refs, "next_" + kind + which) for kind in KINDS)
+        left_stack, right_stack = outer_product(
+            getattr(refs, "basis_" + which)[...], getattr(refs, "new_f_" + which)[...]
+        )
+        for strip in range(weight.shape[0] // rows):
+            at = slice(strip * rows, (strip + 1) * rows)
+            approx = mm_tn(left_stack[:, at], right_stack)
+            new_error[at, :] = error[at, :] - approx
+            send(new_error.at[pl.ds(strip * rows, rows)], getattr(refs, "hbm_err_" + which).at[0, pl.ds(strip * rows, rows)])
+            next_momentum = DECAY * momentum[at, :] + approx
+            new_momentum[at, :] = next_momentum
+            send(new_momentum.at[pl.ds(strip * rows, rows)], getattr(refs, "hbm_mom_" + which).at[pl.ds(strip * rows, rows)])
+            new_weight[at, :] = weight[at, :] - RATE * next_momentum
+            send(new_weight.at[pl.ds(strip * rows, rows)], getattr(refs, "hbm_new_" + which).at[pl.ds(strip * rows, rows)])
     for copy in copies:
         copy.wait()
 
@@ -769,6 +808,12 @@
         raw_special_up=pltpu.VMEM((images, 2, width), BF16),
         mixed=pltpu.VMEM((half, images, width), F32),
         rank=pltpu.VMEM((images, half), jnp.int32),
+        count=pltpu.SMEM((images,), jnp.int32),
+        folded=pltpu.VMEM((rows, 2 * RANK), F32),
+        folded_red=pltpu.VMEM((RANK, rows), BF16),
+        low_probs=pltpu.VMEM((HEADS // 2, 2 * KEYS, 2 * block), BF16),
+        grad_probs=pltpu.VMEM((HEADS // 2, 2 * KEYS, 2 * block), F32),
+        branch_sum=pltpu.VMEM((1, width), F32),
         flags=pltpu.VMEM((8, KEYS), F32),
         other_flags=pltpu.VMEM((8, KEYS), F32),
         mask_columns=pltpu.VMEM((images, 2 * KEYS, 1), F32),
@@ -779,9 +824,9 @@
         scale_two=pltpu.VMEM((rows, 1), F32),
         hidden_one=pltpu.VMEM((rows, width), BF16),
         hidden_two=pltpu.VMEM((rows, width), BF16),
-        low_in=pltpu.VMEM((width, 3 * width), BF16),
-        low_out=pltpu.VMEM((width, width), BF16),
-        low_exp=pltpu.VMEM((width, wide), BF16),
+        low_in=pltpu.VMEM((width + 2 * RANK, 3 * width), BF16),
+        low_out=pltpu.VMEM((width + 2 * RANK, width), BF16),
+        low_exp=pltpu.VMEM((width + 2 * RANK, wide), BF16),
         low_red=pltpu.VMEM((wide, width), BF16),
         query=pltpu.VMEM((rows, width), BF16),
         keys=pltpu.VMEM((2, images, KEYS, 2 * width), BF16),
@@ -825,27 +870,23 @@
         right_in_out=pltpu.VMEM((2 * RANK, width), BF16),
         right_in_slots=pltpu.VMEM((chips, 2 * RANK, width), BF16),
         right_in_total=pltpu.VMEM((4,) + unit, F32),
-        basis_red=pltpu.VMEM((RANK, wide), F32),
-        basis_exp=pltpu.VMEM(unit, F32),
-        basis_out=pltpu.VMEM(unit, F32),
         late_rows=pltpu.VMEM(unit, F32),
-        load_sem=pltpu.SemaphoreType.DMA((23,)),
+        load_sem=pltpu.SemaphoreType.DMA((len(INPUTS),)),
         pair_send=pltpu.SemaphoreType.DMA((13,)),
         pair_recv=pltpu.SemaphoreType.DMA((13,)),
         chip_send=pltpu.SemaphoreType.DMA((6, chips)),
         chip_recv=pltpu.SemaphoreType.DMA((6, chips)),
     )
-    names = INPUTS + OUTPUTS + tuple(scratch)
-    in_specs = [
-        pl.BlockSpec(memory_space=pltpu.SMEM if name == "keep_count" else pl.ANY)
-        for name in INPUTS
-    ]
+    made = OUTPUTS + BASES
+    made_shapes = out_shapes + [((RANK, size), F32) for size in (width, width, width, wide)]
+    names = INPUTS + made + tuple(scratch)
+    in_hbm = pl.BlockSpec(memory_space=pltpu.HBM)
     in_vmem = pl.BlockSpec(memory_space=pltpu.VMEM)
     results = pl.pallas_call(
         functools.partial(layer_kernel, chips, groups, images, half, names),
-        out_shape=[pltpu.VMEM(shape, dtype) for shape, dtype in out_shapes],
-        in_specs=in_specs,
-        out_specs=[in_vmem] * len(OUTPUTS),
+        out_shape=[pltpu.VMEM(shape, dtype) for shape, dtype in made_shapes],
+        in_specs=[in_hbm] * len(INPUTS),
+        out_specs=[in_vmem] * len(made),
         scratch_shapes=list(scratch.values()),
         compiler_params=pltpu.CompilerParams(
             collective_id=0, has_side_effects=True, vmem_limit_bytes=40 << 20
@@ -856,15 +897,24 @@
         jax.ShapeDtypeStruct((1,) + shape if 14 <= index < 18 else shape, dtype)
         for index, (shape, dtype) in enumerate(out_shapes)
     ]
-    count = len(OUTPUTS)
+    updated = {
+        "next_" + kind + which: shape
+        for index, kind in enumerate(KINDS)
+        for which, shape in zip(MATRICES, weight_shapes)
+    }
     stored = list(
         pl.pallas_call(
-            functools.partial(store_kernel, count),
+            functools.partial(
+                store_kernel,
+                made + tuple("hbm_" + name for name in OUTPUTS) + tuple(updated) + ("sem",),
+                OUTPUTS,
+            ),
             out_shape=final_shapes,
-            in_specs=[in_vmem] * count,
-            out_specs=[pl.BlockSpec(memory_space=pl.ANY)] * count,
-            scratch_shapes=[pltpu.SemaphoreType.DMA((count,))],
-            compiler_params=pltpu.CompilerParams(vmem_limit_bytes=1 << 20),
+            in_specs=[in_vmem] * len(made),
+            out_specs=[in_hbm] * len(OUTPUTS),
+            scratch_shapes=[pltpu.VMEM(shape, F32) for shape in updated.values()]
+            + [pltpu.SemaphoreType.DMA((96,))],
+            compiler_params=pltpu.CompilerParams(vmem_limit_bytes=24 << 20),
             name="store",
         )(*results)
     )

time: 60.5 us -> 56.6 us (0.936)
  Pallas kernels: 59.5 us -> 55.6 us
    pallas_call x1, Pallas kernels: 51.9 us -> 47.2 us  [body(): pl.pallas_call(functools.partial(layer_kernel, chips, groups, images, hal...]
    pallas_call x1, Pallas kernels: 7.67 us -> 8.42 us  [body(): pl.pallas_call(functools.partial(store_kernel, made + tuple(('hbm_' + nam...]
where the time goes in v2:
time: 56.6 us; the launch traced here: 56.5 us
  Pallas kernels  55.6 us (98%)
  between operations  0.84 us (1%)
    pallas_call x1, Pallas kernels, body(): pl.pallas_call(functools.partial(layer_kernel, chips, groups, images, hal...  47.2 us
    pallas_call x1, Pallas kernels, body(): pl.pallas_call(functools.partial(store_kernel, made + tuple(('hbm_' + nam...  8.42 us

profile of v2, /device:TPU:0, one launch (start us, length us, event | category | flops | bytes accessed | tf_op | source)
XLA Modules:
  0.0 56.5 jit_solution(2030945636303240273)
XLA Ops:
  0.7 47.2 %layer.1 = (bf16[98,4,384]{2,1,0:T(4,128)(2,1)S(1)}, bf16[4,2,384]{2,1,0:T(2,128)(2,1)S(1)}, bf16[98,4,384]{2,1,0:T(4,128)(2,1)S(1)}, bf16[4,2,384]{2,1,0:T(2,12...) custom-call(bf16[98,4,384]{2,1,0:T(4,128)(2,1)} %bitcast.12, ...), custom_call_target="tpu_custom_call" | custom-call | tf_op jit(solution)/shard_map/layer/pallas_call | solution.py:885
  47.9 8.4 %store.1 = (bf16[98,4,384]{2,1,0:T(4,128)(2,1)}, bf16[4,2,384]{2,1,0:T(2,128)(2,1)}, bf16[98,4,384]{2,1,0:T(4,128)(2,1)}, bf16[4,2,384]{2,1,0:T(2,128)(2,1)}, f3...) custom-call(bf16[98,4,384]{2,1,0:T(4,128)(2,1)S(1)} %get-tuple-eleme, ...), custom_call_target="tpu_custom_call" | custom-call | tf_op jit(solution)/shard_map/store/pallas_call | solution.py:906

commit v3 on v2

--- a/solution.py
+++ b/solution.py
@@ -143,10 +143,20 @@
     partner = 1 - seq
 
     loads = {}
+    free_sems = list(range(r.load_sem.shape[0]))
+
+    class Load:
+        def __init__(self, source, target):
+            self.sem_id = free_sems.pop(0)
+            self.copy = pltpu.make_async_copy(source, target, r.load_sem.at[self.sem_id])
+            self.copy.start()
+
+        def wait(self):
+            self.copy.wait()
+            free_sems.append(self.sem_id)
 
     def load(name, source, target):
-        loads[name] = pltpu.make_async_copy(source, target, r.load_sem.at[len(loads)])
-        loads[name].start()
+        loads[name] = Load(source, target)
 
     load("tokens", r.patch_tokens, r.raw_patch)
     load("special", r.special_tokens, r.raw_special)
@@ -155,17 +165,16 @@
     load("small", r.small_params, r.new_small)
     load("w_in", r.project_in, r.new_in)
 
-    def load_second():
-        load("upstream", r.patch_upstream, r.raw_up)
-        load("special_up", r.special_upstream, r.raw_special_up)
-        load("f_in", r.project_in_factor, r.new_f_in)
-        load("f_out", r.project_out_factor, r.new_f_out)
-        load("f_exp", r.expand_factor, r.new_f_exp)
-        load("f_red", r.reduce_factor, r.new_f_red)
-        load("e_in", r.project_in_error.at[0], r.err_in)
-        load("e_exp", r.expand_error.at[0], r.err_exp)
-        load("e_red", r.reduce_error.at[0], r.err_red)
-        load("e_out", r.project_out_error.at[0], r.err_out)
+    load("f_in", r.project_in_factor, r.new_f_in)
+    load("f_out", r.project_out_factor, r.new_f_out)
+    load("f_exp", r.expand_factor, r.new_f_exp)
+    load("f_red", r.reduce_factor, r.new_f_red)
+    load("upstream", r.patch_upstream, r.raw_up)
+    load("special_up", r.special_upstream, r.raw_special_up)
+    load("e_in", r.project_in_error.at[0], r.err_in)
+    load("e_exp", r.expand_error.at[0], r.err_exp)
+    load("e_red", r.reduce_error.at[0], r.err_red)
+    load("e_out", r.project_out_error.at[0], r.err_out)
 
     def load_third():
         load("w_out", r.project_out, r.new_out)
@@ -182,21 +191,24 @@
     barrier = pltpu.get_barrier_semaphore()
     pl.semaphore_signal(barrier, inc=1, device_id={"seq": partner}, device_id_type=MESH)
 
-    def peer_of(step):
-        other = lax.rem(chip + step, chips)
-        return other // groups, lax.rem(other, groups)
-
-    def greet(step, carry):
-        other_node, other_group = peer_of(step)
-        pl.semaphore_signal(
-            barrier,
-            inc=1,
-            device_id={"node": other_node, "group": other_group},
-            device_id_type=MESH,
-        )
-        return carry
-
-    lax.fori_loop(1, chips, greet, 0)
+    nodes = chips // groups
+
+    def each_chip(act):
+        def row(step, first):
+            for ahead in range(first, groups):
+                act({"node": lax.rem(node + step, nodes), "group": lax.rem(group + ahead, groups)})
+
+        def others(step, carry):
+            row(step, 0)
+            return carry
+
+        lax.fori_loop(1, nodes, others, 0)
+        row(0, 1)
+
+    def greet(device):
+        pl.semaphore_signal(barrier, inc=1, device_id=device, device_id_type=MESH)
+
+    each_chip(greet)
 
     def to_partner(source, target, sem_id):
         return pltpu.make_async_remote_copy(
@@ -208,73 +220,48 @@
             device_id_type=MESH,
         )
 
-    def to_chip(step, source, target, sems, sem_id):
-        other_node, other_group = peer_of(step)
+    def remote(source, target, sem_id, device):
         return pltpu.make_async_remote_copy(
             src_ref=source,
             dst_ref=target,
-            send_sem=sems[0].at[sem_id, step],
-            recv_sem=sems[1].at[sem_id, step],
-            device_id={"node": other_node, "group": other_group},
+            send_sem=r.stage_send.at[sem_id],
+            recv_sem=r.stage_recv.at[sem_id],
+            device_id=device,
             device_id_type=MESH,
         )
 
-    chip_sems = (r.chip_send, r.chip_recv)
+    def stage_finish(count, slots, sem_id):
+        several = slots.at[pl.ds(0, count - 1)]
+        whole = remote(several, several, sem_id, {"seq": partner})
+        whole.wait_recv()
+        whole.wait_send()
+        if count <= 32:
+            total = slots[0].astype(F32)
+            for index in range(1, count):
+                total = total + slots[index].astype(F32)
+            return total
+
+        def add(index, total):
+            return total + slots[index].astype(F32)
+
+        return lax.fori_loop(1, count, add, slots[0].astype(F32))
 
     def chips_start(source, slots, sem_id):
         slots[chip] = source[...]
-
-        def go(step, carry):
-            to_chip(step, source, slots.at[chip], chip_sems, sem_id).start()
-            return carry
-
-        lax.fori_loop(1, chips, go, 0)
-
-    def chips_finish(source, slots, sem_id):
-        def done(step, carry):
-            to_chip(step, source, slots.at[chip], chip_sems, sem_id).wait()
-            return carry
-
-        lax.fori_loop(1, chips, done, 0)
-
-        def add(index, total):
-            return total + slots[index].astype(F32)
-
-        return lax.fori_loop(1, chips, add, slots[0].astype(F32), unroll=min(chips - 1, 15))
-
-    def along(axis, step):
-        size = lax.axis_size(axis)
-        return {axis: lax.rem(lax.axis_index(axis) + step, size)}
-
-    def axis_copy(axis, step, source, slots, sem_id):
-        return pltpu.make_async_remote_copy(
-            src_ref=source,
-            dst_ref=slots.at[lax.axis_index(axis)],
-            send_sem=r.chip_send.at[sem_id, step],
-            recv_sem=r.chip_recv.at[sem_id, step],
-            device_id=along(axis, step),
-            device_id_type=MESH,
-        )
+        each_chip(lambda device: remote(source, slots.at[chip], sem_id, device).start())
+
+    def chips_finish(slots, sem_id):
+        return stage_finish(chips, slots, sem_id)
 
     def axis_start(axis, source, slots, sem_id):
-        slots[lax.axis_index(axis)] = source[...]
-
-        def go(step, carry):
-            axis_copy(axis, step, source, slots, sem_id).start()
-            return carry
-
-        lax.fori_loop(1, lax.axis_size(axis), go, 0)
-
-    def axis_finish(axis, source, slots, sem_id):
-        def done(step, carry):
-            axis_copy(axis, step, source, slots, sem_id).wait()
-            return carry
-
-        lax.fori_loop(1, lax.axis_size(axis), done, 0)
-        total = slots[0].astype(F32)
-        for index in range(1, lax.axis_size(axis)):
-            total = total + slots[index].astype(F32)
-        return total
+        size, place = lax.axis_size(axis), lax.axis_index(axis)
+        slots[place] = source[...]
+        for step in range(1, size):
+            device = {axis: lax.rem(place + step, size)}
+            remote(source, slots.at[place], sem_id, device).start()
+
+    def axis_finish(axis, slots, sem_id):
+        return stage_finish(lax.axis_size(axis), slots, sem_id)
 
     loads["rank"].wait()
     loads["count"].wait()
@@ -324,7 +311,7 @@
         normalise(r.tokens, i, small_row(0), small_row(1), r.xhat_one, r.scale_one, r.hidden_one)
 
     loads["w_in"].wait()
-    load_second()
+    load_third()
     r.low_in[0:width, :] = r.new_in[...].astype(BF16)
     for i in range(images):
         r.keys[0, i, block:KEYS, :] = jnp.zeros((KEYS - block, 2 * width), BF16)
@@ -386,7 +373,6 @@
     r.left_in[...] = error_left(r.err_in, r.new_f_in, 0, width)
     loads["e_exp"].wait()
     r.lefts[4] = error_left(r.err_exp, r.new_f_exp, 0, width)
-    load_third()
     loads["e_red"].wait()
     for part in range(4):
         r.lefts[part] = error_left(r.err_red, r.new_f_red, part * width, width)
@@ -446,7 +432,7 @@
     def _(i):
         normalise(r.middle, i, small_row(5), small_row(6), r.xhat_two, r.scale_two, r.hidden_two)
 
-    strip = 16
+    strip = 64
     chunk = 2 * width
     hidden_lanes = r.low_exp.shape[1]
     loads["w_exp"].wait()
@@ -454,24 +440,38 @@
     loads["w_red"].wait()
     r.low_red[...] = r.new_red[...].astype(BF16)
     bias_rows = chunk // width
+    part_lanes = r.wide.shape[2]
+    parts = hidden_lanes // part_lanes
+    bias_one = jnp.concatenate([small_row(8 + index) for index in range(hidden_lanes // width)], axis=1)
     r.total[...] = r.middle[...] + small_row(7)
-    for part in range(hidden_lanes // chunk):
-        lanes = slice(part * chunk, (part + 1) * chunk)
-        bias = jnp.concatenate(
-            [small_row(8 + part * bias_rows + index) for index in range(bias_rows)], axis=1
-        )
-        r.wide[...] = mm(r.hidden_two[...], r.low_exp[0:width, lanes])
-
-        @pl.loop(0, rows_all // strip)
-        def _(index):
-            at = pl.ds(pl.multiple_of(index * strip, strip), strip)
-            pre = r.wide[at, :] + bias
+
+    def lanes_at(part, count=1):
+        return slice(part * part_lanes, (part + count) * part_lanes)
+
+    def expand(part):
+        r.wide[part % 2] = mm(r.hidden_two[...], r.low_exp[0:width, lanes_at(part)])
+
+    def activate(part):
+        for index in range(rows_all // strip):
+            at = slice(index * strip, (index + 1) * strip)
+            pre = r.wide[part % 2, at, :] + bias_one[:, lanes_at(part)]
             normal = 0.5 + 0.5 * lax.erf(pre * (1.0 / math.sqrt(2.0)))
             density = jnp.exp(-0.5 * pre * pre) * (1.0 / math.sqrt(2.0 * math.pi))
-            r.activated[at, lanes] = (pre * normal).astype(BF16)
-            r.slope[at, lanes] = normal + pre * density
-
+            r.activated[at, lanes_at(part)] = (pre * normal).astype(BF16)
+            r.slope[at, lanes_at(part)] = normal + pre * density
+
+    def contract(part):
+        lanes = lanes_at(part, 2)
         r.total[...] += mm(r.activated[:, lanes], r.low_red[lanes, :])
+
+    expand(0)
+    for part in range(parts):
+        if part + 1 < parts:
+            expand(part + 1)
+        activate(part)
+        if part >= 2 and part % 2 == 0:
+            contract(part - 2)
+    contract(parts - 2)
     for i in range(images):
         base = i * block
         r.mixed[:, i, :] = r.total[base : base + half, :]
@@ -553,12 +553,12 @@
         axis_start("group", outgoing.at[0], slots, sem_id)
 
     def units_node_start(outgoing, group_slots, node_slots, sem_id):
-        total = axis_finish("group", outgoing.at[0], group_slots, sem_id)
+        total = axis_finish("group", group_slots, sem_id)
         outgoing[1] = total.astype(BF16)
         axis_start("node", outgoing.at[1], node_slots, sem_id + 1)
 
-    def units_share(outgoing, node_slots, result, sem_id, pair_id):
-        total = axis_finish("node", outgoing.at[1], node_slots, sem_id)
+    def units_share(node_slots, result, sem_id, pair_id):
+        total = axis_finish("node", node_slots, sem_id)
         for index in range(2):
             first = seq * 4 + 2 * index
             result[first] = total[index, 0:RANK]
@@ -616,6 +616,10 @@
     row_ids = lax.broadcasted_iota(jnp.int32, (block, 1), 0)
     halved = jnp.where((row_ids >= special) & (row_ids < special + 2), 0.5, 1.0)
     r.late_rows[...] = jnp.zeros_like(r.late_rows)
+    r.err_out[...] += mm_tn(r.attended[...], r.grad_branch[...])
+    for part in range(hidden_lanes // chunk):
+        lanes = slice(part * chunk, (part + 1) * chunk)
+        r.err_red[lanes, :] += mm_tn(r.activated[:, lanes], r.upstream[...])
 
     @pl.loop(0, images)
     def _(i):
@@ -638,7 +642,17 @@
     r.left_in[...] += left_of(r.hidden_one)
     left_in_copy = to_partner(r.left_in, r.left_in_arrived, 4)
     left_in_copy.start()
-
+    r.gain_sum[...] = jnp.zeros_like(r.gain_sum)
+    r.shift_sum[...] = jnp.zeros_like(r.shift_sum)
+
+    @pl.loop(0, images)
+    def _(i):
+        at = pl.ds(pl.multiple_of(i * block, 16), block)
+        back = normalise_back(i, small_row(0), r.xhat_one, r.scale_one, r.gain_sum, r.shift_sum)
+        r.total[at, :] = (back + r.grad_middle[at, :]) * jnp.where(halved < 1.0, 2.0, 1.0)
+
+    r.late_rows[0:1, :] = r.gain_sum[...]
+    r.late_rows[1:2, :] = r.shift_sum[...]
     left_in_copy.wait()
     pair_sum = r.left_in[...] + r.left_in_arrived[...]
     r.left_in_out[...] = jnp.concatenate(
@@ -647,23 +661,10 @@
     ).astype(BF16)
     chips_start(r.left_in_out, r.left_in_slots, 5)
 
-    r.err_out[...] += mm_tn(r.attended[...], r.grad_branch[...])
+    left_share = units_share(r.lefts_node, r.lefts_total, 1, 3)
     for part in range(hidden_lanes // chunk):
         lanes = slice(part * chunk, (part + 1) * chunk)
-        r.err_red[lanes, :] += mm_tn(r.activated[:, lanes], r.upstream[...])
         r.err_exp[:, lanes] += mm_tn(r.hidden_two[...], r.grad_pre[:, lanes])
-    left_share = units_share(r.lefts_out, r.lefts_node, r.lefts_total, 1, 3)
-    r.gain_sum[...] = jnp.zeros_like(r.gain_sum)
-    r.shift_sum[...] = jnp.zeros_like(r.shift_sum)
-
-    @pl.loop(0, images)
-    def _(i):
-        at = pl.ds(pl.multiple_of(i * block, 16), block)
-        back = normalise_back(i, small_row(0), r.xhat_one, r.scale_one, r.gain_sum, r.shift_sum)
-        r.total[at, :] = (back + r.grad_middle[at, :]) * jnp.where(halved < 1.0, 2.0, 1.0)
-
-    r.late_rows[0:1, :] = r.gain_sum[...]
-    r.late_rows[1:2, :] = r.shift_sum[...]
     left_share.wait()
     inverse = 1.0 / workers
     basis_red = orthonormal(
@@ -693,7 +694,7 @@
         r.err_in[:, lanes] += mm_tn(r.hidden_one[...], r.grad_qkv[:, lanes])
     units_group_start(right_copy, r.rights, r.rights_arrived, r.rights_out, r.rights_group, 2)
 
-    total = chips_finish(r.left_in_out, r.left_in_slots, 5)
+    total = chips_finish(r.left_in_slots, 5)
     basis_in = orthonormal(
         jnp.concatenate([total[0:RANK], total[RANK : 2 * RANK, 0:128]], axis=1) * inverse
     )
@@ -723,7 +724,7 @@
 
     for name in ("m_small", "m_in", "m_out", "m_exp", "m_red"):
         loads[name].wait()
-    right_share = units_share(r.rights_out, r.rights_node, r.rights_total, 3, 7)
+    right_share = units_share(r.rights_node, r.rights_total, 3, 7)
     right_share.wait()
     for part in range(4):
         r.new_f_exp[:, part * width : (part + 1) * width] = r.rights_total[part] * inverse
@@ -737,7 +738,7 @@
 
     small_update(slice(4, 12), r.lefts_total[6])
 
-    total = chips_finish(r.right_in_out, r.right_in_slots, 4)
+    total = chips_finish(r.right_in_slots, 4)
     r.right_in_total[first] = total[0:RANK]
     r.right_in_total[first + 1] = total[RANK : 2 * RANK]
     half_units = r.right_in_total.at[pl.ds(first, 2)]
@@ -753,18 +754,27 @@
     refs = Names()
     for name, ref in zip(names, all_refs):
         setattr(refs, name, ref)
-    copies = []
-
-    def send(source, target):
-        copies.append(pltpu.make_async_copy(source, target, refs.sem.at[len(copies)]))
-        copies[-1].start()
+    waits = []
+
+    def send(name, at=None):
+        source, target = getattr(refs, "next_" + name, None), getattr(refs, "hbm_" + name)
+        if source is None:
+            source = getattr(refs, name)
+        if len(target.shape) > len(source.shape):
+            target = target.at[0]
+        sem = refs.sem.at[targets.index(name)]
+        if at is None or at.start == 0:
+            waits.append(pltpu.make_async_copy(source, target, sem))
+        if at is not None:
+            at = pl.ds(at.start, at.stop - at.start)
+            source, target = source.at[at], target.at[at]
+        pltpu.make_async_copy(source, target, sem).start()
 
     updated = {kind + which for kind in KINDS for which in MATRICES}
     for name in targets:
         if name not in updated:
-            send(getattr(refs, name), getattr(refs, "hbm_" + name))
-    rows = 128
-    for which in ("exp", "red", "out", "in"):
+            send(name)
+    for which, rows in (("exp", 128), ("red", 384), ("out", 384), ("in", 128)):
         weight, momentum, error = (getattr(refs, kind + which) for kind in KINDS)
         new_weight, new_momentum, new_error = (getattr(refs, "next_" + kind + which) for kind in KINDS)
         left_stack, right_stack = outer_product(
@@ -774,13 +784,13 @@
             at = slice(strip * rows, (strip + 1) * rows)
             approx = mm_tn(left_stack[:, at], right_stack)
             new_error[at, :] = error[at, :] - approx
-            send(new_error.at[pl.ds(strip * rows, rows)], getattr(refs, "hbm_err_" + which).at[0, pl.ds(strip * rows, rows)])
+            send("err_" + which, at)
             next_momentum = DECAY * momentum[at, :] + approx
             new_momentum[at, :] = next_momentum
-            send(new_momentum.at[pl.ds(strip * rows, rows)], getattr(refs, "hbm_mom_" + which).at[pl.ds(strip * rows, rows)])
+            send("mom_" + which, at)
             new_weight[at, :] = weight[at, :] - RATE * next_momentum
-            send(new_weight.at[pl.ds(strip * rows, rows)], getattr(refs, "hbm_new_" + which).at[pl.ds(strip * rows, rows)])
-    for copy in copies:
+            send("new_" + which, at)
+    for copy in waits:
         copy.wait()
 
 
@@ -834,7 +844,7 @@
         probs=pltpu.VMEM((images * HEADS // 2, 2 * KEYS, 2 * block), F32),
         attended=pltpu.VMEM((rows, width), BF16),
         middle=pltpu.VMEM((rows, width), F32),
-        wide=pltpu.VMEM((rows, 2 * width), F32),
+        wide=pltpu.VMEM((2, rows, 256), F32),
         activated=pltpu.VMEM((rows, wide), BF16),
         slope=pltpu.VMEM((rows, wide), F32),
         grad_pre=pltpu.VMEM((rows, wide), BF16),
@@ -871,11 +881,11 @@
         right_in_slots=pltpu.VMEM((chips, 2 * RANK, width), BF16),
         right_in_total=pltpu.VMEM((4,) + unit, F32),
         late_rows=pltpu.VMEM(unit, F32),
-        load_sem=pltpu.SemaphoreType.DMA((len(INPUTS),)),
+        load_sem=pltpu.SemaphoreType.DMA((16,)),
         pair_send=pltpu.SemaphoreType.DMA((13,)),
         pair_recv=pltpu.SemaphoreType.DMA((13,)),
-        chip_send=pltpu.SemaphoreType.DMA((6, chips)),
-        chip_recv=pltpu.SemaphoreType.DMA((6, chips)),
+        stage_send=pltpu.SemaphoreType.DMA((6,)),
+        stage_recv=pltpu.SemaphoreType.DMA((6,)),
     )
     made = OUTPUTS + BASES
     made_shapes = out_shapes + [((RANK, size), F32) for size in (width, width, width, wide)]
@@ -913,7 +923,7 @@
             in_specs=[in_vmem] * len(made),
             out_specs=[in_hbm] * len(OUTPUTS),
             scratch_shapes=[pltpu.VMEM(shape, F32) for shape in updated.values()]
-            + [pltpu.SemaphoreType.DMA((96,))],
+            + [pltpu.SemaphoreType.DMA((len(OUTPUTS),))],
             compiler_params=pltpu.CompilerParams(vmem_limit_bytes=24 << 20),
             name="store",
         )(*results)

time: 56.6 us -> 52.7 us (0.931)
  Pallas kernels: 55.6 us -> 51.7 us
    pallas_call x1, Pallas kernels: 47.2 us -> 43.9 us  [body(): pl.pallas_call(functools.partial(layer_kernel, chips, groups, images, hal...]
    pallas_call x1, Pallas kernels: 8.42 us -> 7.76 us  [body(): pl.pallas_call(functools.partial(store_kernel, made + tuple(('hbm_' + nam...]
where the time goes in v3:
time: 52.7 us; the launch traced here: 52.5 us
  Pallas kernels  51.7 us (98%)
  between operations  0.84 us (2%)
    pallas_call x1, Pallas kernels, body(): pl.pallas_call(functools.partial(layer_kernel, chips, groups, images, hal...  43.9 us
    pallas_call x1, Pallas kernels, body(): pl.pallas_call(functools.partial(store_kernel, made + tuple(('hbm_' + nam...  7.76 us

profile of v3, /device:TPU:0, one launch (start us, length us, event | category | flops | bytes accessed | tf_op | source)
XLA Modules:
  0.0 52.5 jit_solution(11871891784161162102)
XLA Ops:
  0.7 43.9 %layer.1 = (bf16[98,4,384]{2,1,0:T(4,128)(2,1)S(1)}, bf16[4,2,384]{2,1,0:T(2,128)(2,1)S(1)}, bf16[98,4,384]{2,1,0:T(4,128)(2,1)S(1)}, bf16[4,2,384]{2,1,0:T(2,12...) custom-call(bf16[98,4,384]{2,1,0:T(4,128)(2,1)} %bitcast.12, ...), custom_call_target="tpu_custom_call" | custom-call | tf_op jit(solution)/shard_map/layer/pallas_call | solution.py:895
  44.6 7.8 %store.1 = (bf16[98,4,384]{2,1,0:T(4,128)(2,1)}, bf16[4,2,384]{2,1,0:T(2,128)(2,1)}, bf16[98,4,384]{2,1,0:T(4,128)(2,1)}, bf16[4,2,384]{2,1,0:T(2,128)(2,1)}, f3...) custom-call(bf16[98,4,384]{2,1,0:T(4,128)(2,1)S(1)} %get-tuple-eleme, ...), custom_call_target="tpu_custom_call" | custom-call | tf_op jit(solution)/shard_map/store/pallas_call | solution.py:916

commit v4 on v3

--- a/solution.py
+++ b/solution.py
@@ -131,6 +131,7 @@
     for name, ref in zip(names, all_refs):
         setattr(refs, name, ref)
     r = refs
+    r.grad_middle, r.grad_query = r.tokens, r.middle
     width = HEADS * HEAD_DIM
     special = round_up(half, 8)
     block = round_up(special + 2, 16)
@@ -311,30 +312,24 @@
         normalise(r.tokens, i, small_row(0), small_row(1), r.xhat_one, r.scale_one, r.hidden_one)
 
     loads["w_in"].wait()
-    load_third()
     r.low_in[0:width, :] = r.new_in[...].astype(BF16)
     for i in range(images):
         r.keys[0, i, block:KEYS, :] = jnp.zeros((KEYS - block, 2 * width), BF16)
-    for part in (1, 2, 0):
-        product = mm(r.hidden_one[...], r.low_in[0:width, part * width : (part + 1) * width])
-        if part == 0:
-            query = (product + small_row(2)).astype(BF16).astype(F32) * (
-                1.0 / math.sqrt(HEAD_DIM)
-            )
-            r.query[...] = query.astype(BF16)
-        else:
-            if part == 2:
-                product = product + small_row(3)
-            for i in range(images):
-                r.keys[0, i, 0:block, (part - 1) * width : part * width] = product[
-                    i * block : (i + 1) * block
-                ].astype(BF16)
-        if part == 2:
-            pl.semaphore_wait(barrier, chips)
-            key_copy = to_partner(r.keys.at[0], r.keys.at[1], 0)
-            flag_copy = to_partner(r.flags, r.other_flags, 1)
-            key_copy.start()
-            flag_copy.start()
+    product = mm(r.hidden_one[...], r.low_in[0:width, width : 3 * width])
+    for i in range(images):
+        at = slice(i * block, (i + 1) * block)
+        r.keys[0, i, 0:block, 0:width] = product[at, 0:width].astype(BF16)
+        r.keys[0, i, 0:block, width : 2 * width] = (
+            product[at, width : 2 * width] + small_row(3)
+        ).astype(BF16)
+    pl.semaphore_wait(barrier, chips)
+    key_copy = to_partner(r.keys.at[0], r.keys.at[1], 0)
+    flag_copy = to_partner(r.flags, r.other_flags, 1)
+    key_copy.start()
+    flag_copy.start()
+    product = mm(r.hidden_one[...], r.low_in[0:width, 0:width])
+    query = (product + small_row(2)).astype(BF16).astype(F32) * (1.0 / math.sqrt(HEAD_DIM))
+    r.query[...] = query.astype(BF16)
 
     def error_left(error_ref, factor_ref, row_start, row_count):
         return mm_nt(
@@ -373,6 +368,7 @@
     r.left_in[...] = error_left(r.err_in, r.new_f_in, 0, width)
     loads["e_exp"].wait()
     r.lefts[4] = error_left(r.err_exp, r.new_f_exp, 0, width)
+    load_third()
     loads["e_red"].wait()
     for part in range(4):
         r.lefts[part] = error_left(r.err_red, r.new_f_red, part * width, width)
@@ -401,27 +397,35 @@
     def of_both(i, lanes):
         return jnp.concatenate([r.keys[0, i, :, lanes], r.keys[1, i, :, lanes]], axis=0)
 
-    @pl.loop(0, images)
-    def _(i):
-        at = pl.ds(pl.multiple_of(i * block, 16), block)
-        valid = r.mask_columns[i] > 0.5
-
-        def lanes_of(pair, first=0):
-            return slice(first + pair * pair_width, first + (pair + 1) * pair_width)
-
-        for pair in range(pairs):
-            scores = mm_nt(of_both(i, lanes_of(pair)), stacked(r.query[at, lanes_of(pair)]))
-            r.probs[i * pairs + pair] = jnp.where(valid, scores, -1e30)
-        for pair in range(pairs):
+    together = 2
+
+    def lanes_of(pair, first=0):
+        return slice(first + pair * pair_width, first + (pair + 1) * pair_width)
+
+    def image_rows(i):
+        return pl.ds(pl.multiple_of(i * block, 16), block)
+
+    tasks = [(ahead, pair) for ahead in range(together) for pair in range(pairs)]
+
+    @pl.loop(0, images // together)
+    def _(step):
+        for ahead, pair in tasks:
+            i = step * together + ahead
+            queries = stacked(r.query[image_rows(i), lanes_of(pair)])
+            scores = mm_nt(of_both(i, lanes_of(pair)), queries)
+            r.probs[i * pairs + pair] = jnp.where(r.mask_columns[i] > 0.5, scores, -1e30)
+        for task, (ahead, pair) in enumerate(tasks):
+            i = step * together + ahead
             scores = r.probs[i * pairs + pair]
             top = jnp.max(scores, axis=0, keepdims=True)
             weights = jnp.exp(scores - top)
             probs = weights * (1.0 / jnp.sum(weights, axis=0, keepdims=True))
             r.probs[i * pairs + pair] = probs
-            r.low_probs[pair] = probs.astype(BF16)
-        for pair in range(pairs):
-            mixed = mm_tn(r.low_probs[pair], of_both(i, lanes_of(pair, width)))
-            r.attended[at, lanes_of(pair)] = unstacked(mixed).astype(BF16)
+            r.low_probs[task] = probs.astype(BF16)
+        for task, (ahead, pair) in enumerate(tasks):
+            i = step * together + ahead
+            mixed = mm_tn(r.low_probs[task], of_both(i, lanes_of(pair, width)))
+            r.attended[image_rows(i), lanes_of(pair)] = unstacked(mixed).astype(BF16)
 
     loads["w_out"].wait()
     load_last()
@@ -478,6 +482,36 @@
         r.out_special[i] = r.total[base + special : base + special + 2, :].astype(BF16)
 
     r.out_patch[...] = r.mixed[...].astype(BF16)
+
+    def units_pair_start(units, arrived, sem_id):
+        copy = to_partner(units, arrived, sem_id)
+        copy.start()
+        return copy
+
+    def units_group_start(copy, units, arrived, outgoing, slots, sem_id):
+        copy.wait()
+        for index in range(2):
+            first = seq * 4 + 2 * index
+            outgoing[0, index] = jnp.concatenate(
+                [units[first] + arrived[first], units[first + 1] + arrived[first + 1]], axis=0
+            ).astype(BF16)
+        axis_start("group", outgoing.at[0], slots, sem_id)
+
+    def units_node_start(outgoing, group_slots, node_slots, sem_id):
+        total = axis_finish("group", group_slots, sem_id)
+        outgoing[1] = total.astype(BF16)
+        axis_start("node", outgoing.at[1], node_slots, sem_id + 1)
+
+    def units_share(node_slots, result, sem_id, pair_id):
+        total = axis_finish("node", node_slots, sem_id)
+        for index in range(2):
+            first = seq * 4 + 2 * index
+            result[first] = total[index, 0:RANK]
+            result[first + 1] = total[index, RANK : 2 * RANK]
+        half_units = result.at[pl.ds(seq * 4, 4)]
+        copy = to_partner(half_units, half_units, pair_id)
+        copy.start()
+        return copy
 
     for part in range(4):
         lanes = slice(part * width, (part + 1) * width)
@@ -538,88 +572,67 @@
     r.folded[...] = back[:, width : width + 2 * RANK]
     r.lefts[5] += left_of(r.attended)
 
-    def units_pair_start(units, arrived, sem_id):
-        copy = to_partner(units, arrived, sem_id)
-        copy.start()
-        return copy
-
-    def units_group_start(copy, units, arrived, outgoing, slots, sem_id):
-        copy.wait()
-        for index in range(2):
-            first = seq * 4 + 2 * index
-            outgoing[0, index] = jnp.concatenate(
-                [units[first] + arrived[first], units[first + 1] + arrived[first + 1]], axis=0
-            ).astype(BF16)
-        axis_start("group", outgoing.at[0], slots, sem_id)
-
-    def units_node_start(outgoing, group_slots, node_slots, sem_id):
-        total = axis_finish("group", group_slots, sem_id)
-        outgoing[1] = total.astype(BF16)
-        axis_start("node", outgoing.at[1], node_slots, sem_id + 1)
-
-    def units_share(node_slots, result, sem_id, pair_id):
-        total = axis_finish("node", node_slots, sem_id)
-        for index in range(2):
-            first = seq * 4 + 2 * index
-            result[first] = total[index, 0:RANK]
-            result[first + 1] = total[index, RANK : 2 * RANK]
-        half_units = result.at[pl.ds(seq * 4, 4)]
-        copy = to_partner(half_units, half_units, pair_id)
-        copy.start()
-        return copy
-
     left_copy = units_pair_start(r.lefts, r.lefts_arrived, 2)
 
     def grad_copy(i):
         return to_partner(r.grad_sent.at[i], r.grad_arrived.at[i], 8 + i)
 
-    @pl.loop(0, images)
-    def _(i):
-        base = pl.multiple_of(i * block, 16)
-        at = pl.ds(base, block)
-        specials = pl.ds(pl.multiple_of(base + special, 8), 2)
-
-        def lanes_of(pair, first=0):
-            return slice(first + pair * pair_width, first + (pair + 1) * pair_width)
-
-        for pair in range(pairs):
-            grad_mixed = stacked(r.grad_attended[at, lanes_of(pair)])
-            r.grad_probs[pair] = mm_nt(of_both(i, lanes_of(pair, width)), grad_mixed)
-        for pair in range(pairs):
+    def scratch_at(task):
+        return slice(0, 2 * KEYS), slice(task * 2 * KEYS, task * 2 * KEYS + 2 * block)
+
+    def special_rows(i):
+        return pl.ds(pl.multiple_of(i * block + special, 8), 2)
+
+    def reduce_gradient(part):
+        lanes = slice(part * chunk, (part + 1) * chunk)
+        r.err_red[lanes, :] += mm_tn(r.activated[:, lanes], r.upstream[...])
+
+    def expand_gradient(part):
+        lanes = slice(part * chunk, (part + 1) * chunk)
+        r.err_exp[:, lanes] += mm_tn(r.hidden_two[...], r.grad_pre[:, lanes])
+
+    r.err_out[...] += mm_tn(r.attended[...], r.grad_branch[...])
+    reduce_gradient(0)
+    units_group_start(left_copy, r.lefts, r.lefts_arrived, r.lefts_out, r.lefts_group, 0)
+
+    @pl.loop(0, images // together)
+    def _(step):
+        for task, (ahead, pair) in enumerate(tasks):
+            i = step * together + ahead
+            grad_mixed = stacked(r.grad_attended[image_rows(i), lanes_of(pair)])
+            r.slope[scratch_at(task)] = mm_nt(of_both(i, lanes_of(pair, width)), grad_mixed)
+        for task, (ahead, pair) in enumerate(tasks):
+            i = step * together + ahead
             probs = r.probs[i * pairs + pair]
-            weighted = probs * r.grad_probs[pair]
+            weighted = probs * r.slope[scratch_at(task)]
             delta = jnp.sum(weighted, axis=0, keepdims=True)
-            r.low_probs[pair] = (weighted - probs * delta).astype(BF16)
-        for pair in range(pairs):
-            grad_scores = r.low_probs[pair]
-            r.grad_query[at, lanes_of(pair)] = unstacked(
-                mm_tn(grad_scores, of_both(i, lanes_of(pair)))
-            ) * (1.0 / math.sqrt(HEAD_DIM))
-            grad_keys = mm(grad_scores, stacked(r.query[at, lanes_of(pair)]))
-            r.grad_own[i, :, lanes_of(pair)] = grad_keys[0:KEYS]
-            r.grad_sent[i, :, lanes_of(pair)] = grad_keys[KEYS : 2 * KEYS]
-        for pair in range(pairs):
-            grad_mixed = stacked(r.grad_attended[at, lanes_of(pair)])
-            grad_values = mm(r.probs[i * pairs + pair].astype(BF16), grad_mixed)
-            r.grad_own[i, :, lanes_of(pair, width)] = grad_values[0:KEYS]
-            r.grad_sent[i, :, lanes_of(pair, width)] = grad_values[KEYS : 2 * KEYS]
-        r.grad_sent[i, special : special + 2, :] = r.grad_own[i, special : special + 2, :]
-        r.grad_sent[i, block : block + 2, 0:width] = r.grad_query[specials, :]
-        grad_copy(i).start()
-
-        @pl.when(i == 0)
-        def _():
-            units_group_start(left_copy, r.lefts, r.lefts_arrived, r.lefts_out, r.lefts_group, 0)
-
-    units_node_start(r.lefts_out, r.lefts_group, r.lefts_node, 0)
+            r.low_probs[task] = (weighted - probs * delta).astype(BF16)
+        for ahead in range(together):
+            i = step * together + ahead
+            at = image_rows(i)
+            for pair in range(pairs):
+                grad_scores = r.low_probs[ahead * pairs + pair]
+                r.grad_query[at, lanes_of(pair)] = unstacked(
+                    mm_tn(grad_scores, of_both(i, lanes_of(pair)))
+                ) * (1.0 / math.sqrt(HEAD_DIM))
+                grad_keys = mm(grad_scores, stacked(r.query[at, lanes_of(pair)]))
+                r.grad_own[i, :, lanes_of(pair)] = grad_keys[0:KEYS]
+                r.grad_sent[i, :, lanes_of(pair)] = grad_keys[KEYS : 2 * KEYS]
+            for pair in range(pairs):
+                grad_mixed = stacked(r.grad_attended[at, lanes_of(pair)])
+                grad_values = mm(r.probs[i * pairs + pair].astype(BF16), grad_mixed)
+                r.grad_own[i, :, lanes_of(pair, width)] = grad_values[0:KEYS]
+                r.grad_sent[i, :, lanes_of(pair, width)] = grad_values[KEYS : 2 * KEYS]
+            r.grad_sent[i, special : special + 2, :] = r.grad_own[i, special : special + 2, :]
+            r.grad_sent[i, block : block + 2, 0:width] = r.grad_query[special_rows(i), :]
+            grad_copy(i).start()
 
     row_ids = lax.broadcasted_iota(jnp.int32, (block, 1), 0)
     halved = jnp.where((row_ids >= special) & (row_ids < special + 2), 0.5, 1.0)
     r.late_rows[...] = jnp.zeros_like(r.late_rows)
-    r.err_out[...] += mm_tn(r.attended[...], r.grad_branch[...])
-    for part in range(hidden_lanes // chunk):
-        lanes = slice(part * chunk, (part + 1) * chunk)
-        r.err_red[lanes, :] += mm_tn(r.activated[:, lanes], r.upstream[...])
+    for part in range(1, hidden_lanes // chunk):
+        reduce_gradient(part)
+    expand_gradient(0)
 
     @pl.loop(0, images)
     def _(i):
@@ -636,23 +649,13 @@
         r.late_rows[3:4, :] += jnp.sum(rest[:, width : 2 * width], axis=0, keepdims=True)
         r.grad_qkv[at, width : 3 * width] = rest.astype(BF16)
 
-    back = mm_nt(r.grad_qkv[...], r.low_in[...])
-    r.total[...] = back[:, 0:width]
-    r.folded[...] = back[:, width : width + 2 * RANK]
+    units_node_start(r.lefts_out, r.lefts_group, r.lefts_node, 0)
+
+    r.folded[...] = mm_nt(r.grad_qkv[...], r.low_in[width : width + 2 * RANK, :])
     r.left_in[...] += left_of(r.hidden_one)
     left_in_copy = to_partner(r.left_in, r.left_in_arrived, 4)
     left_in_copy.start()
-    r.gain_sum[...] = jnp.zeros_like(r.gain_sum)
-    r.shift_sum[...] = jnp.zeros_like(r.shift_sum)
-
-    @pl.loop(0, images)
-    def _(i):
-        at = pl.ds(pl.multiple_of(i * block, 16), block)
-        back = normalise_back(i, small_row(0), r.xhat_one, r.scale_one, r.gain_sum, r.shift_sum)
-        r.total[at, :] = (back + r.grad_middle[at, :]) * jnp.where(halved < 1.0, 2.0, 1.0)
-
-    r.late_rows[0:1, :] = r.gain_sum[...]
-    r.late_rows[1:2, :] = r.shift_sum[...]
+    r.total[...] = mm_nt(r.grad_qkv[...], r.low_in[0:width, :])
     left_in_copy.wait()
     pair_sum = r.left_in[...] + r.left_in_arrived[...]
     r.left_in_out[...] = jnp.concatenate(
@@ -661,10 +664,32 @@
     ).astype(BF16)
     chips_start(r.left_in_out, r.left_in_slots, 5)
 
+    for part in range(1, hidden_lanes // chunk):
+        expand_gradient(part)
+    r.gain_sum[...] = jnp.zeros_like(r.gain_sum)
+    r.shift_sum[...] = jnp.zeros_like(r.shift_sum)
+
+    @pl.loop(0, images)
+    def _(i):
+        at = pl.ds(pl.multiple_of(i * block, 16), block)
+        back = normalise_back(i, small_row(0), r.xhat_one, r.scale_one, r.gain_sum, r.shift_sum)
+        r.total[at, :] = (back + r.grad_middle[at, :]) * jnp.where(halved < 1.0, 2.0, 1.0)
+
+    r.late_rows[0:1, :] = r.gain_sum[...]
+    r.late_rows[1:2, :] = r.shift_sum[...]
     left_share = units_share(r.lefts_node, r.lefts_total, 1, 3)
-    for part in range(hidden_lanes // chunk):
-        lanes = slice(part * chunk, (part + 1) * chunk)
-        r.err_exp[:, lanes] += mm_tn(r.hidden_two[...], r.grad_pre[:, lanes])
+    for part in range(3):
+        lanes = slice(part * width, (part + 1) * width)
+        r.err_in[:, lanes] += mm_tn(r.hidden_one[...], r.grad_qkv[:, lanes])
+    own_lanes = r.cross_arrived.shape[1]
+    apart = 3 * width - own_lanes
+    cross_sent = r.low_exp.at[pl.ds(0, width), pl.ds(0, own_lanes)]
+    cross_own = r.low_exp.at[pl.ds(0, width), pl.ds(own_lanes, own_lanes)]
+    cross_sent[...] = r.err_in[:, pl.ds(pl.multiple_of(partner * apart, 128), own_lanes)].astype(
+        BF16
+    )
+    cross_copy = to_partner(cross_sent, r.cross_arrived, 6)
+    cross_copy.start()
     left_share.wait()
     inverse = 1.0 / workers
     basis_red = orthonormal(
@@ -686,45 +711,34 @@
         r.rights[part] = right_of(basis_exp, r.err_exp[:, lanes])
     r.rights[4] = right_of(basis_red, r.err_red[...])
     r.rights[5] = right_of(basis_out, r.err_out[...])
-    r.rights[6] = jnp.zeros((RANK, width), F32)
+    r.rights[6] = r.late_rows[...]
     r.rights[7] = jnp.zeros((RANK, width), F32)
     right_copy = units_pair_start(r.rights, r.rights_arrived, 5)
-    for part in range(3):
-        lanes = slice(part * width, (part + 1) * width)
-        r.err_in[:, lanes] += mm_tn(r.hidden_one[...], r.grad_qkv[:, lanes])
     units_group_start(right_copy, r.rights, r.rights_arrived, r.rights_out, r.rights_group, 2)
+    cross_own[...] = r.err_in[:, pl.ds(pl.multiple_of(seq * apart, 128), own_lanes)].astype(BF16)
 
     total = chips_finish(r.left_in_slots, 5)
     basis_in = orthonormal(
         jnp.concatenate([total[0:RANK], total[RANK : 2 * RANK, 0:128]], axis=1) * inverse
     )
     r.basis_in[...] = basis_in
-    for part in range(3):
-        lanes = slice(part * width, (part + 1) * width)
-        r.right_in[part] = right_of(basis_in, r.err_in[:, lanes])
-    r.right_in[3] = r.late_rows[...]
-    right_in_copy = to_partner(r.right_in, r.right_in_arrived, 6)
-    right_in_copy.start()
+    cross_copy.wait()
+    part = right_of(basis_in, cross_own[...]) + right_of(basis_in, r.cross_arrived[...])
+    rest = jnp.concatenate(
+        [part[:, width:own_lanes], jnp.zeros((RANK, 2 * width - own_lanes), F32)], axis=1
+    )
+    r.right_in_out[...] = jnp.concatenate([part[:, 0:width], rest], axis=0).astype(BF16)
+    chips_start(r.right_in_out, r.right_in_slots, 4)
+    units_node_start(r.rights_out, r.rights_group, r.rights_node, 2)
     for i in range(images):
         base = i * block
         r.mixed[:, i, :] = r.total[base : base + half, :] * r.mask_columns[i, 0:half, :]
         r.grad_special[i] = r.total[base + special : base + special + 2, :].astype(BF16)
-    right_in_copy.wait()
-    first = seq * 2
-    r.right_in_out[...] = jnp.concatenate(
-        [
-            r.right_in[first] + r.right_in_arrived[first],
-            r.right_in[first + 1] + r.right_in_arrived[first + 1],
-        ],
-        axis=0,
-    ).astype(BF16)
-    chips_start(r.right_in_out, r.right_in_slots, 4)
-    units_node_start(r.rights_out, r.rights_group, r.rights_node, 2)
     r.grad_patch[...] = r.mixed[...].astype(BF16)
 
     for name in ("m_small", "m_in", "m_out", "m_exp", "m_red"):
         loads[name].wait()
-    right_share = units_share(r.rights_node, r.rights_total, 3, 7)
+    right_share = units_share(r.rights_node, r.rights_total, 3, 12)
     right_share.wait()
     for part in range(4):
         r.new_f_exp[:, part * width : (part + 1) * width] = r.rights_total[part] * inverse
@@ -736,18 +750,20 @@
         r.mom_small[at, :] = momentum
         r.new_small[at, :] = r.new_small[at, :] - RATE * momentum
 
+    small_update(slice(0, 4), r.rights_total[6][0:4])
     small_update(slice(4, 12), r.lefts_total[6])
 
     total = chips_finish(r.right_in_slots, 4)
-    r.right_in_total[first] = total[0:RANK]
-    r.right_in_total[first + 1] = total[RANK : 2 * RANK]
-    half_units = r.right_in_total.at[pl.ds(first, 2)]
-    share = to_partner(half_units, half_units, 12)
+    r.right_in_total[seq] = jnp.concatenate(
+        [total[0:RANK], total[RANK : 2 * RANK, 0 : own_lanes - width]], axis=1
+    )
+    share = to_partner(r.right_in_total.at[seq], r.right_in_total.at[seq], 7)
     share.start()
     share.wait()
-    for part in range(3):
-        r.new_f_in[:, part * width : (part + 1) * width] = r.right_in_total[part] * inverse
-    small_update(slice(0, 4), r.right_in_total[3][0:4])
+    r.new_f_in[:, 0:own_lanes] = r.right_in_total[0] * inverse
+    r.new_f_in[:, own_lanes : 3 * width] = (
+        r.right_in_total[1][:, 2 * own_lanes - 3 * width : own_lanes] * inverse
+    )
 
 
 def store_kernel(names, targets, *all_refs):
@@ -811,6 +827,7 @@
     out_shapes += [(shape, F32) for shape in weight_shapes]
     out_shapes += [((RANK, size), F32) for size in (3 * width, width, wide, width)]
     unit = (RANK, width)
+    own_lanes = round_up(3 * width // 2, 128)
     scratch = dict(
         raw_patch=pltpu.VMEM((half, images, width), BF16),
         raw_special=pltpu.VMEM((images, 2, width), BF16),
@@ -821,8 +838,7 @@
         count=pltpu.SMEM((images,), jnp.int32),
         folded=pltpu.VMEM((rows, 2 * RANK), F32),
         folded_red=pltpu.VMEM((RANK, rows), BF16),
-        low_probs=pltpu.VMEM((HEADS // 2, 2 * KEYS, 2 * block), BF16),
-        grad_probs=pltpu.VMEM((HEADS // 2, 2 * KEYS, 2 * block), F32),
+        low_probs=pltpu.VMEM((HEADS, 2 * KEYS, 2 * block), BF16),
         branch_sum=pltpu.VMEM((1, width), F32),
         flags=pltpu.VMEM((8, KEYS), F32),
         other_flags=pltpu.VMEM((8, KEYS), F32),
@@ -851,10 +867,8 @@
         total=pltpu.VMEM((rows, width), F32),
         gain_sum=pltpu.VMEM((1, width), F32),
         shift_sum=pltpu.VMEM((1, width), F32),
-        grad_middle=pltpu.VMEM((rows, width), F32),
         grad_branch=pltpu.VMEM((rows, width), BF16),
         grad_attended=pltpu.VMEM((rows, width), BF16),
-        grad_query=pltpu.VMEM((rows, width), F32),
         grad_own=pltpu.VMEM((images, KEYS, 2 * width), F32),
         grad_sent=pltpu.VMEM((images, KEYS, 2 * width), F32),
         grad_arrived=pltpu.VMEM((images, KEYS, 2 * width), F32),
@@ -875,15 +889,14 @@
         left_in_arrived=pltpu.VMEM(unit, F32),
         left_in_out=pltpu.VMEM((2 * RANK, 256), BF16),
         left_in_slots=pltpu.VMEM((chips, 2 * RANK, 256), BF16),
-        right_in=pltpu.VMEM((4,) + unit, F32),
-        right_in_arrived=pltpu.VMEM((4,) + unit, F32),
+        cross_arrived=pltpu.VMEM((width, own_lanes), BF16),
         right_in_out=pltpu.VMEM((2 * RANK, width), BF16),
         right_in_slots=pltpu.VMEM((chips, 2 * RANK, width), BF16),
-        right_in_total=pltpu.VMEM((4,) + unit, F32),
+        right_in_total=pltpu.VMEM((2, RANK, own_lanes), F32),
         late_rows=pltpu.VMEM(unit, F32),
         load_sem=pltpu.SemaphoreType.DMA((16,)),
-        pair_send=pltpu.SemaphoreType.DMA((13,)),
-        pair_recv=pltpu.SemaphoreType.DMA((13,)),
+        pair_send=pltpu.SemaphoreType.DMA((15,)),
+        pair_recv=pltpu.SemaphoreType.DMA((15,)),
         stage_send=pltpu.SemaphoreType.DMA((6,)),
         stage_recv=pltpu.SemaphoreType.DMA((6,)),
     )

time: 52.7 us -> 50.6 us (0.960)
  Pallas kernels: 51.7 us -> 49.6 us
    pallas_call x1, Pallas kernels: 43.9 us -> 41.8 us  [body(): pl.pallas_call(functools.partial(layer_kernel, chips, groups, images, hal...]
where the time goes in v4:
time: 50.6 us; the launch traced here: 50.4 us
  Pallas kernels  49.6 us (98%)
  between operations  0.84 us (2%)
    pallas_call x1, Pallas kernels, body(): pl.pallas_call(functools.partial(layer_kernel, chips, groups, images, hal...  41.8 us
    pallas_call x1, Pallas kernels, body(): pl.pallas_call(functools.partial(store_kernel, made + tuple(('hbm_' + nam...  7.77 us

profile of v4, /device:TPU:0, one launch (start us, length us, event | category | flops | bytes accessed | tf_op | source)
XLA Modules:
  0.0 50.4 jit_solution(11761441554679155360)
XLA Ops:
  0.7 41.8 %layer.1 = (bf16[98,4,384]{2,1,0:T(4,128)(2,1)S(1)}, bf16[4,2,384]{2,1,0:T(2,128)(2,1)S(1)}, bf16[98,4,384]{2,1,0:T(4,128)(2,1)S(1)}, bf16[4,2,384]{2,1,0:T(2,12...) custom-call(bf16[98,4,384]{2,1,0:T(4,128)(2,1)} %bitcast.12, ...), custom_call_target="tpu_custom_call" | custom-call | tf_op jit(solution)/shard_map/layer/pallas_call | solution.py:908
  42.5 7.8 %store.1 = (bf16[98,4,384]{2,1,0:T(4,128)(2,1)}, bf16[4,2,384]{2,1,0:T(2,128)(2,1)}, bf16[98,4,384]{2,1,0:T(4,128)(2,1)}, bf16[4,2,384]{2,1,0:T(2,128)(2,1)}, f3...) custom-call(bf16[98,4,384]{2,1,0:T(4,128)(2,1)S(1)} %get-tuple-eleme, ...), custom_call_target="tpu_custom_call" | custom-call | tf_op jit(solution)/shard_map/store/pallas_call | solution.py:929

commit v5 on v4

--- a/solution.py
+++ b/solution.py
@@ -164,7 +164,8 @@
     load("rank", r.patch_rank, r.rank)
     load("count", r.keep_count, r.count)
     load("small", r.small_params, r.new_small)
-    load("w_in", r.project_in, r.new_in)
+    for name, lanes in (("w_keys", pl.ds(width, 2 * width)), ("w_query", pl.ds(0, width))):
+        load(name, r.project_in.at[:, lanes], r.new_in.at[:, lanes])
 
     load("f_in", r.project_in_factor, r.new_f_in)
     load("f_out", r.project_out_factor, r.new_f_out)
@@ -311,8 +312,8 @@
     def _(i):
         normalise(r.tokens, i, small_row(0), small_row(1), r.xhat_one, r.scale_one, r.hidden_one)
 
-    loads["w_in"].wait()
-    r.low_in[0:width, :] = r.new_in[...].astype(BF16)
+    loads["w_keys"].wait()
+    r.low_in[0:width, width : 3 * width] = r.new_in[:, width : 3 * width].astype(BF16)
     for i in range(images):
         r.keys[0, i, block:KEYS, :] = jnp.zeros((KEYS - block, 2 * width), BF16)
     product = mm(r.hidden_one[...], r.low_in[0:width, width : 3 * width])
@@ -327,6 +328,8 @@
     flag_copy = to_partner(r.flags, r.other_flags, 1)
     key_copy.start()
     flag_copy.start()
+    loads["w_query"].wait()
+    r.low_in[0:width, 0:width] = r.new_in[:, 0:width].astype(BF16)
     product = mm(r.hidden_one[...], r.low_in[0:width, 0:width])
     query = (product + small_row(2)).astype(BF16).astype(F32) * (1.0 / math.sqrt(HEAD_DIM))
     r.query[...] = query.astype(BF16)
@@ -738,32 +741,31 @@
 
     for name in ("m_small", "m_in", "m_out", "m_exp", "m_red"):
         loads[name].wait()
+    total = chips_finish(r.right_in_slots, 4)
+    r.right_in_total[seq] = jnp.concatenate(
+        [total[0:RANK], total[RANK : 2 * RANK, 0 : own_lanes - width]], axis=1
+    )
+    share = to_partner(r.right_in_total.at[seq], r.right_in_total.at[seq], 7)
+    share.start()
     right_share = units_share(r.rights_node, r.rights_total, 3, 12)
+
+    def small_update(at, grad):
+        momentum = DECAY * r.mom_small[at, :] + grad * inverse
+        r.mom_small[at, :] = momentum
+        r.new_small[at, :] = r.new_small[at, :] - RATE * momentum
+
+    small_update(slice(4, 12), r.lefts_total[6])
+    share.wait()
+    r.new_f_in[:, 0:own_lanes] = r.right_in_total[0] * inverse
+    r.new_f_in[:, own_lanes : 3 * width] = (
+        r.right_in_total[1][:, 2 * own_lanes - 3 * width : own_lanes] * inverse
+    )
     right_share.wait()
     for part in range(4):
         r.new_f_exp[:, part * width : (part + 1) * width] = r.rights_total[part] * inverse
     r.new_f_red[...] = r.rights_total[4] * inverse
     r.new_f_out[...] = r.rights_total[5] * inverse
-
-    def small_update(at, grad):
-        momentum = DECAY * r.mom_small[at, :] + grad * inverse
-        r.mom_small[at, :] = momentum
-        r.new_small[at, :] = r.new_small[at, :] - RATE * momentum
-
     small_update(slice(0, 4), r.rights_total[6][0:4])
-    small_update(slice(4, 12), r.lefts_total[6])
-
-    total = chips_finish(r.right_in_slots, 4)
-    r.right_in_total[seq] = jnp.concatenate(
-        [total[0:RANK], total[RANK : 2 * RANK, 0 : own_lanes - width]], axis=1
-    )
-    share = to_partner(r.right_in_total.at[seq], r.right_in_total.at[seq], 7)
-    share.start()
-    share.wait()
-    r.new_f_in[:, 0:own_lanes] = r.right_in_total[0] * inverse
-    r.new_f_in[:, own_lanes : 3 * width] = (
-        r.right_in_total[1][:, 2 * own_lanes - 3 * width : own_lanes] * inverse
-    )
 
 
 def store_kernel(names, targets, *all_refs):
@@ -894,7 +896,7 @@
         right_in_slots=pltpu.VMEM((chips, 2 * RANK, width), BF16),
         right_in_total=pltpu.VMEM((2, RANK, own_lanes), F32),
         late_rows=pltpu.VMEM(unit, F32),
-        load_sem=pltpu.SemaphoreType.DMA((16,)),
+        load_sem=pltpu.SemaphoreType.DMA((17,)),
         pair_send=pltpu.SemaphoreType.DMA((15,)),
         pair_recv=pltpu.SemaphoreType.DMA((15,)),
         stage_send=pltpu.SemaphoreType.DMA((6,)),

time: 50.6 us -> 50.3 us (level)
  no operation moved by 1% of the time
where the time goes in v5:
time: 50.3 us; the launch traced here: 50.1 us
  Pallas kernels  49.3 us (98%)
  between operations  0.84 us (2%)
    pallas_call x1, Pallas kernels, body(): pl.pallas_call(functools.partial(layer_kernel, chips, groups, images, hal...  41.5 us
    pallas_call x1, Pallas kernels, body(): pl.pallas_call(functools.partial(store_kernel, made + tuple(('hbm_' + nam...  7.76 us

profile of v5, /device:TPU:0, one launch (start us, length us, event | category | flops | bytes accessed | tf_op | source)
XLA Modules:
  0.0 50.1 jit_solution(17201869516544207427)
XLA Ops:
  0.7 41.5 %layer.1 = (bf16[98,4,384]{2,1,0:T(4,128)(2,1)S(1)}, bf16[4,2,384]{2,1,0:T(2,128)(2,1)S(1)}, bf16[98,4,384]{2,1,0:T(4,128)(2,1)S(1)}, bf16[4,2,384]{2,1,0:T(2,12...) custom-call(bf16[98,4,384]{2,1,0:T(4,128)(2,1)} %bitcast.12, ...), custom_call_target="tpu_custom_call" | custom-call | tf_op jit(solution)/shard_map/layer/pallas_call | solution.py:910
  42.2 7.8 %store.1 = (bf16[98,4,384]{2,1,0:T(4,128)(2,1)}, bf16[4,2,384]{2,1,0:T(2,128)(2,1)}, bf16[98,4,384]{2,1,0:T(4,128)(2,1)}, bf16[4,2,384]{2,1,0:T(2,128)(2,1)}, f3...) custom-call(bf16[98,4,384]{2,1,0:T(4,128)(2,1)S(1)} %get-tuple-eleme, ...), custom_call_target="tpu_custom_call" | custom-call | tf_op jit(solution)/shard_map/store/pallas_call | solution.py:931

commit v6 on v5

--- a/solution.py
+++ b/solution.py
@@ -792,7 +792,7 @@
     for name in targets:
         if name not in updated:
             send(name)
-    for which, rows in (("exp", 128), ("red", 384), ("out", 384), ("in", 128)):
+    for which, rows in (("exp", 64), ("in", 64), ("red", 256), ("out", 192)):
         weight, momentum, error = (getattr(refs, kind + which) for kind in KINDS)
         new_weight, new_momentum, new_error = (getattr(refs, "next_" + kind + which) for kind in KINDS)
         left_stack, right_stack = outer_product(
@@ -897,8 +897,8 @@
         right_in_total=pltpu.VMEM((2, RANK, own_lanes), F32),
         late_rows=pltpu.VMEM(unit, F32),
         load_sem=pltpu.SemaphoreType.DMA((17,)),
-        pair_send=pltpu.SemaphoreType.DMA((15,)),
-        pair_recv=pltpu.SemaphoreType.DMA((15,)),
+        pair_send=pltpu.SemaphoreType.DMA((13,)),
+        pair_recv=pltpu.SemaphoreType.DMA((13,)),
         stage_send=pltpu.SemaphoreType.DMA((6,)),
         stage_recv=pltpu.SemaphoreType.DMA((6,)),
     )

time: 50.3 us -> 50.1 us (level)
  no operation moved by 1% of the time
where the time goes in v6:
time: 50.1 us; the launch traced here: 49.9 us
  Pallas kernels  49.1 us (98%)
  between operations  0.84 us (2%)
    pallas_call x1, Pallas kernels, body(): pl.pallas_call(functools.partial(layer_kernel, chips, groups, images, hal...  41.5 us
    pallas_call x1, Pallas kernels, body(): pl.pallas_call(functools.partial(store_kernel, made + tuple(('hbm_' + nam...  7.62 us

profile of v6, /device:TPU:0, one launch (start us, length us, event | category | flops | bytes accessed | tf_op | source)
XLA Modules:
  0.0 49.9 jit_solution(6087656886109662714)
XLA Ops:
  0.7 41.5 %layer.1 = (bf16[98,4,384]{2,1,0:T(4,128)(2,1)S(1)}, bf16[4,2,384]{2,1,0:T(2,128)(2,1)S(1)}, bf16[98,4,384]{2,1,0:T(4,128)(2,1)S(1)}, bf16[4,2,384]{2,1,0:T(2,12...) custom-call(bf16[98,4,384]{2,1,0:T(4,128)(2,1)} %bitcast.12, ...), custom_call_target="tpu_custom_call" | custom-call | tf_op jit(solution)/shard_map/layer/pallas_call | solution.py:910
  42.1 7.6 %store.1 = (bf16[98,4,384]{2,1,0:T(4,128)(2,1)}, bf16[4,2,384]{2,1,0:T(2,128)(2,1)}, bf16[98,4,384]{2,1,0:T(4,128)(2,1)}, bf16[4,2,384]{2,1,0:T(2,128)(2,1)}, f3...) custom-call(bf16[98,4,384]{2,1,0:T(4,128)(2,1)S(1)} %get-tuple-eleme, ...), custom_call_target="tpu_custom_call" | custom-call | tf_op jit(solution)/shard_map/store/pallas_call | solution.py:931
